TPU v7x, 256 devices: a whole 4x4x8 slice. The times are simulated.
256 devices in a mesh: seq: 32 (over z_hi, y, core), tp: 8 (over z_lo, x).
Axes of the slice: x: 4, y: 4, z: 8 (z_hi: 4, z_lo: 2; z = z_hi * 2 + z_lo), core: 2. Of those that a mesh axis runs over, the one named last changes fastest.
Arguments:
- hidden_in: bfloat16 [16384, 4608], P('seq', 'tp'), may hold values from -6 to 6
- pre_gain: float32 [4608], replicated, may hold values from 0.1 to 1.9
- post_gain: float32 [4608], replicated, may hold values from 0.1 to 1.9
- w_query: bfloat16 [4608, 2048], P(None, 'tp'), may hold values from -0.4375 to 0.4375
- key_weight: bfloat16 [4608, 1024], P(None, 'tp'), may hold values from -0.21875 to 0.21875
- value_weight: bfloat16 [4608, 1024], P(None, 'tp'), may hold values from -0.21875 to 0.21875
- w_out: bfloat16 [2048, 4608], P(None, 'tp'), may hold values from -0.125 to 0.125
- prefix_key_value_cache: bfloat16 [65536, 2, 1024], P('seq', None, 'tp'), may hold values from -15 to 15
- suffix_len: int32 [48], replicated, may hold values from 1 to 2048, 16384 in all
- request_order: int32 [48], replicated, may hold values from 0 to 47, each once
- request_prefix: int32 [48], replicated, may hold values from 0 to 3
- prefix_owner: int32 [4], replicated, may hold values from 0 to 31, as said below
Outputs:
- hidden_out: bfloat16 [16384, 4608], P('seq', 'tp')
Inputs may be any that keep to these rules, and one draw needn't show every extreme that they name: `suffix_len`: the suffix lengths sum to 16384, and the longest is exactly 2048. `request_order`: every request appears exactly once. `prefix_owner`: the 4 owners are distinct, and the first and the last index of seq are among them.
All inputs are finite; a program needn't handle non-finite values.
Results may differ from a plain program's by a relative error of at most 0.011.
Values may be sent and summed in bfloat16 or wider, within the bound.
A program may use at most 128 MiB of HBM per device.

v0:
```python
import jax
import jax.numpy as jnp
from jax import lax
from jax.sharding import PartitionSpec as P

MODEL_WIDTH = 4608
HEAD_SIZE = 128
QSCALE = 144
PREFIX_LENGTH = 2048
NPRE = 4
REACH = 4


softcap = 50.0
rope_base = 10000.0
eps = 1e-06


def passed_along(block, axis, distance):
    devices = range(lax.axis_size(axis))
    route = [(i - distance, i) for i in devices if i - distance in devices]
    return lax.ppermute(block, axis, route)


def spread(array, axis, root):
    mine = lax.axis_index(axis) == root
    return lax.psum(jnp.where(mine, array, jnp.zeros_like(array)), axis)


def request_layout(suffix_len, request_order, request_prefix, token_ids):
    req_count = request_order.shape[0]
    ladder = jnp.arange(req_count, dtype=jnp.int32)
    chosen = (request_order[:, None] == ladder[None, :]).astype(jnp.int32)
    ordered_len = jnp.sum(chosen * suffix_len[None, :], axis=1)
    ordered_prefix = jnp.sum(chosen * request_prefix[None, :], axis=1)
    stop_at = jnp.cumsum(ordered_len)
    starts = stop_at - ordered_len
    slot_ids = jnp.sum((stop_at[None, :] <= token_ids[:, None]).astype(jnp.int32), axis=1)
    member = (slot_ids[:, None] == ladder[None, :]).astype(jnp.int32)
    positions = token_ids - jnp.sum(member * starts[None, :], axis=1)
    prefixes = jnp.sum(member * ordered_prefix[None, :], axis=1)
    return (slot_ids, positions, prefixes)


def apply_rotary(value_rows, positions):
    half_width = value_rows.shape[-1] // 2
    ladder = jnp.arange(half_width, dtype=jnp.float32)
    frequency = rope_base ** (-2.0 * ladder / value_rows.shape[-1])
    angles = positions.astype(jnp.float32)[:, None] * frequency[None, :]
    cosine = jnp.cos(angles)[:, None, :]
    sine_part = jnp.sin(angles)[:, None, :]
    first_half = value_rows[..., :half_width]
    second_half = value_rows[..., half_width:]
    return jnp.concatenate(
        [
            first_half * cosine - second_half * sine_part,
            second_half * cosine + first_half * sine_part,
        ],
        axis=-1,
    )


def attend(query_rows, key_rows, value_rows, allowed):
    scores = jnp.einsum(
        "tkgd,skd->tkgs", query_rows, key_rows, preferred_element_type=jnp.float32
    ) * QSCALE ** (-0.5)
    capped = softcap * jnp.tanh(scores / softcap)
    weights = jnp.where(allowed[:, None, None, :], jnp.exp(capped), 0.0).astype(jnp.bfloat16)
    numerator = jnp.einsum(
        "tkgs,skd->tkgd", weights, value_rows, preferred_element_type=jnp.float32
    )
    softmax_denominator = jnp.sum(weights.astype(jnp.float32), axis=-1)
    return (numerator, softmax_denominator)


def on_device(
    hidden_in,
    pre_gain,
    post_gain,
    w_query,
    key_weight,
    value_weight,
    w_out,
    prefix_key_value_cache,
    suffix_len,
    request_order,
    request_prefix,
    prefix_owner,
):
    tok_count = hidden_in.shape[0]
    seq_index = lax.axis_index("seq")
    tp_index = lax.axis_index("tp")
    token_ids = seq_index * tok_count + jnp.arange(tok_count, dtype=jnp.int32)
    slot_ids, positions, prefixes = request_layout(
        suffix_len, request_order, request_prefix, token_ids
    )
    wide = hidden_in.astype(jnp.float32)
    kv_local = key_weight.shape[1] // HEAD_SIZE
    query_group = w_query.shape[1] // key_weight.shape[1]
    whole = lax.all_gather(hidden_in, "tp", axis=1, tiled=True)
    whole_wide = whole.astype(jnp.float32)
    normed_input = (
        whole_wide
        * lax.rsqrt(jnp.sum(whole_wide * whole_wide, axis=1, keepdims=True) / MODEL_WIDTH + eps)
        * pre_gain[None, :]
    ).astype(jnp.bfloat16)
    query_acc = jnp.dot(normed_input, w_query, preferred_element_type=jnp.float32)
    key_acc = jnp.dot(normed_input, key_weight, preferred_element_type=jnp.float32)
    value_acc = jnp.dot(normed_input, value_weight, preferred_element_type=jnp.float32)
    rotary_position = positions + PREFIX_LENGTH
    query_rows = (
        apply_rotary(
            query_acc.reshape(tok_count, kv_local * query_group, HEAD_SIZE), rotary_position
        )
        .astype(jnp.bfloat16)
        .reshape(tok_count, kv_local, query_group, HEAD_SIZE)
    )
    key_rows = apply_rotary(
        key_acc.reshape(tok_count, kv_local, HEAD_SIZE), rotary_position
    ).astype(jnp.bfloat16)
    value_rows = value_acc.astype(jnp.bfloat16).reshape(tok_count, kv_local, HEAD_SIZE)
    own_pair = jnp.stack([key_rows, value_rows], axis=1)
    pair_list = [own_pair]
    id_list = [token_ids]
    for back in range(1, REACH + 1):
        pair_list.append(passed_along(own_pair, "seq", back))
        id_list.append(token_ids - back * tok_count)
    all_pairs = jnp.concatenate(pair_list, axis=0)
    key_ids = jnp.concatenate(id_list, axis=0)
    key_slot, unused_pos, unused_prefix = request_layout(
        suffix_len, request_order, request_prefix, key_ids
    )
    allowed = (
        (key_ids[None, :] >= 0)
        & (key_ids[None, :] <= token_ids[:, None])
        & (key_slot[None, :] == slot_ids[:, None])
    )
    numerator, softmax_denominator = attend(query_rows, all_pairs[:, 0], all_pairs[:, 1], allowed)
    zero_numer = jnp.zeros((tok_count, kv_local, query_group, HEAD_SIZE), jnp.float32)
    zero_total = jnp.zeros((tok_count, kv_local, query_group), jnp.float32)
    for prefix_idx in range(NPRE):
        cache_kv = spread(prefix_key_value_cache, "seq", prefix_owner[prefix_idx])
        rows = prefixes == prefix_idx
        shaped = cache_kv.reshape(cache_kv.shape[0], 2, kv_local, HEAD_SIZE)

        def compute_part():
            return attend(query_rows, shaped[:, 0], shaped[:, 1], rows[:, None])

        def skip_part():
            return (zero_numer, zero_total)

        part_numer, part_total = lax.cond(jnp.any(rows), compute_part, skip_part)
        numerator = numerator + part_numer
        softmax_denominator = softmax_denominator + part_total
    attended = (
        (numerator / softmax_denominator[..., None])
        .astype(jnp.bfloat16)
        .reshape(tok_count, kv_local * query_group * HEAD_SIZE)
    )
    out_cols = w_out.shape[1]
    projected = jnp.dot(
        lax.all_gather(attended, "tp", axis=1, tiled=True),
        w_out,
        preferred_element_type=jnp.float32,
    )
    out_sq = lax.psum(jnp.sum(projected * projected, axis=1), "tp")
    local_post = lax.dynamic_slice_in_dim(post_gain, tp_index * out_cols, out_cols)
    post = projected * lax.rsqrt(out_sq / MODEL_WIDTH + eps)[:, None] * local_post[None, :]
    return (wide + post).astype(jnp.bfloat16)


def solution(mesh):
    placed = (
        P("seq", "tp"),
        P(),
        P(),
        P(None, "tp"),
        P(None, "tp"),
        P(None, "tp"),
        P(None, "tp"),
        P("seq", None, "tp"),
        P(),
        P(),
        P(),
        P(),
    )
    return jax.shard_map(
        on_device, mesh=mesh, in_specs=placed, out_specs=P("seq", "tp"), check_vma=False
    )
```

profile of v0, /device:TPU:2, one launch (start us, length us, event | category | flops | bytes accessed | tf_op | source)
XLA Modules:
  0.0 457.1 jit_solution(12125726063546785620)
XLA Ops:
  12.2 3.4 broadcast_select_fusion.3
  16.4 1.8 multiply_cosine_fusion
  21.6 3.5 compare_and_fusion
  25.1 54.4 %all-gather.3.cloned.1.call-done = bf16[512,4608]{0,1:T(8,128)(2,1)} async-done(((bf16[512,576]{0,1:T(8,128)(2,1)}), bf16[512,4608]{0,1:T(8,128)(2,1)}) %all-gather.3.cloned.1.call-update) | async-done | bytes 4718608 | tf_op jit(solution)/shard_map/all_gather | solution.py:100
  79.5 3.5 fusion.29
  83.3 3.2 convolution_bitcast_fusion
  89.7 2.0 collective-permute-start
  91.7 2.0 collective-permute-start.1
  93.7 2.0 collective-permute-start.2
  95.7 9.0 %collective-permute-start.3 = (bf16[512,2,1,128]{0,3,2,1:T(8,128)(2,1)}, bf16[512,2,1,128]{0,3,2,1:T(8,128)(2,1)}, u32[]{:S(2)}, u32[]{:S(2)}) collective-permute-start(bf16[512,2,1,128]{0,3,2,1:T(8,128)(2,1)} %get-tuple-element.99), channel_id=1, source_target_pairs={{0,32},{8,40},{16,48},{24,56},{32,64},{40,72},{48,80},{56,88},{64,... | collective-permute-start | bytes 786440 | tf_op jit(solution)/shard_map/ppermute | solution.py:22
  104.8 1.8 fusion.75
  110.8 247.0 %all-reduce.3.cloned.1.call-done = (bf16[2048,2,128]{2,0,1:T(8,128)(2,1)}, bf16[2048,2,128]{2,0,1:T(8,128)(2,1)}, bf16[2048,2,128]{2,0,1:T(8,128)(2,1)}, bf16[2048,2,128]{2,0,1:T(8,128)(2,1)}) async-done(((bf16[2048,2,128]{2,0,1:T(8,128)(2,1)}, bf16[2048,2,128]{2,0,1:T(8,128)(2,1)}, bf16[2048,2,128]{2,0,1:T(8,128)(2,1)}, bf16[2048,2,128]{2,0,1:T(8,128)(2,1)}), (bf16[2048,2,128]{2,0,1:T(8,128)(2,1)}, ...) | async-done | bytes 4194320 | tf_op jit(solution)/shard_map/psum | solution.py:27
  357.9 4.8 %conditional.7 = (f32[512,1,2]{0,2,1:T(2,128)S(1)}, f32[512,1,2,128]{0,3,2,1:T(8,128)S(1)}) conditional(s32[]{:T(128)} %convert_element_type.107, () %tuple.43, (pred[512]{0:T(512)(128)(4,1)S(1)}, bf16[2048,2,128]{2,0,1:T(8,128)(2,1)}, bf16[512,1,2,128]{3,0,2,1:T(8,128)(2,1)S(1)}) %tuple.44), branch_computations={%region_25.26_spmd, %region_26.28_spmd} | conditional | flops 1086323712 | bytes 14422572 | solution.py:152
  357.9 4.0 convert_reduce_fusion.3
  362.7 4.9 %conditional.6 = (f32[512,1,2]{0,2,1:T(2,128)S(1)}, f32[512,1,2,128]{0,3,2,1:T(8,128)S(1)}) conditional(s32[]{:T(128)} %convert_element_type.106, () %tuple.41, (pred[512]{0:T(512)(128)(4,1)S(1)}, bf16[2048,2,128]{2,0,1:T(8,128)(2,1)}, bf16[512,1,2,128]{3,0,2,1:T(8,128)(2,1)S(1)}) %tuple.42), branch_computations={%region_20.21_spmd, %region_21.23_spmd} | conditional | flops 1086323712 | bytes 14422572 | solution.py:152
  362.8 4.0 convert_reduce_fusion.2
  368.5 4.7 %conditional.4 = (f32[512,1,2]{0,2,1:T(2,128)S(1)}, f32[512,1,2,128]{0,3,2,1:T(8,128)S(1)}) conditional(s32[]{:T(128)} %convert_element_type.104, () %tuple.37, (pred[512]{0:T(512)(128)(4,1)S(1)}, bf16[2048,2,128]{2,0,1:T(8,128)(2,1)}, bf16[512,1,2,128]{3,0,2,1:T(8,128)(2,1)}) %tuple.99), branch_computations={%region_10.11_spmd, %region_11.13_spmd} | conditional | flops 1086323712 | bytes 14422572 | solution.py:152
  368.5 3.7 convert_reduce_fusion
  373.3 1.9 constant_dynamic-update-slice_fusion.3
  380.3 5.6 %convert_reduce_fusion.4 = (f32[512,2]{0,1:T(2,128)S(1)}, bf16[512,1,2,2560]{0,3,2,1:T(8,128)(2,1)S(1)}) fusion(bf16[512,2,64]{2,0,1:T(8,128)(2,1)} %copy-done.8, bf16[512,2,64]{2,0,1:T(8,128)(2,1)} %copy-done.7, bf16[2560,2,1,128]{0,3,2,1:T(8,128)(2,1)} %constant_dynamic-update-slice_fusion, pred[512,2560]{0,1:T(8,128)(4,1)} %compare_and_fusion), kind=kOutput, calls=%fused_computation.40 | convolution fusion | flops 687340544 | bytes 7737344 | tf_op jit(solution)/shard_map/tkgd,skd->tkgs/dot_general | solution.py:64
  388.5 36.1 %all-gather.5.cloned.1.call-done = bf16[512,2048]{0,1:T(8,128)(2,1)} async-done(((bf16[512,256]{0,1:T(8,128)(2,1)}), bf16[512,2048]{0,1:T(8,128)(2,1)}) %all-gather.5.cloned.1.call-update) | async-done | bytes 2097168 | tf_op jit(solution)/shard_map/all_gather | solution.py:162
  424.6 4.0 multiply_reduce_fusion
  428.6 18.7 %psum.39 = f32[512]{0:T(512)S(1)} all-reduce(f32[512]{0:T(512)S(1)} %get-tuple-element.115), channel_id=1, replica_groups=mesh['seq'=32,'tp'=8] {'tp'}, use_global_device_ids=true, to_apply=%region_30.31 | all-reduce | flops 512 | bytes 4096 | tf_op jit(solution)/shard_map/psum | solution.py:166
  447.3 2.3 add_convert_fusion
  (91 shorter events, 22.5 us)
Async XLA Ops:
  7.4 417.2 %copy-start = (bf16[2048,576]{0,1:T(8,128)(2,1)S(1)}, bf16[2048,576]{0,1:T(8,128)(2,1)}, u32[]{:S(2)}) copy-start(bf16[2048,576]{0,1:T(8,128)(2,1)} %param.26) | copy-start | bytes 7077892
  7.4 72.2 %all-gather.3.cloned.1.call-start = ((), (), s32[]{:S(2)}) async-start(), calls=%async_computation | async-start | bytes 5308416 | tf_op jit(solution)/shard_map/all_gather | solution.py:100
  8.1 349.8 %all-reduce.3.cloned.1.call-start = ((), (), s32[]{:S(2)}) async-start(), calls=%async_computation.2 | async-start | bytes 8388608 | tf_op jit(solution)/shard_map/psum | solution.py:27
  12.1 3.5 copy-start.11
  12.1 3.5 copy-start.12
  12.1 3.5 copy-start.13
  15.5 67.5 %copy-start.20 = (f32[4608]{0:T(1024)S(1)}, f32[4608]{0:T(1024)}, u32[]{:S(2)}) copy-start(f32[4608]{0:T(1024)} %param.21) | copy-start | bytes 55300
  15.6 409.0 %all-gather.5.cloned.1.call-start = ((), (), s32[]{:S(2)}) async-start(), calls=%async_computation.1 | async-start | bytes 2359296 | tf_op jit(solution)/shard_map/all_gather | solution.py:162
  79.5 3.8 copy-start.5
  83.3 3.8 copy-start.15
  87.0 17.7 %copy-start.14 = (bf16[4608,256]{1,0:T(8,128)(2,1)S(1)}, bf16[4608,256]{1,0:T(8,128)(2,1)}, u32[]{:S(2)}) copy-start(bf16[4608,256]{1,0:T(8,128)(2,1)} %param.23) | copy-start | bytes 7077892
  89.7 283.5 %collective-permute-start = (bf16[512,2,1,128]{0,3,2,1:T(8,128)(2,1)}, bf16[512,2,1,128]{0,3,2,1:T(8,128)(2,1)}, u32[]{:S(2)}, u32[]{:S(2)}) collective-permute-start(bf16[512,2,1,128]{0,3,2,1:T(8,128)(2,1)} %get-tuple-element.99), channel_id=1, source_target_pairs={{0,8},{8,16},{16,24},{24,32},{32,40},{40,48},{48,56},{56,64},{64,7... | collective-permute-start | bytes 786440 | tf_op jit(solution)/shard_map/ppermute | solution.py:22
  91.7 283.4 %collective-permute-start.1 = (bf16[512,2,1,128]{0,3,2,1:T(8,128)(2,1)}, bf16[512,2,1,128]{0,3,2,1:T(8,128)(2,1)}, u32[]{:S(2)}, u32[]{:S(2)}) collective-permute-start(bf16[512,2,1,128]{0,3,2,1:T(8,128)(2,1)} %get-tuple-element.99), channel_id=1, source_target_pairs={{0,16},{8,24},{16,32},{24,40},{32,48},{40,56},{48,64},{56,72},{64,... | collective-permute-start | bytes 786440 | tf_op jit(solution)/shard_map/ppermute | solution.py:22
  93.7 283.1 %collective-permute-start.2 = (bf16[512,2,1,128]{0,3,2,1:T(8,128)(2,1)}, bf16[512,2,1,128]{0,3,2,1:T(8,128)(2,1)}, u32[]{:S(2)}, u32[]{:S(2)}) collective-permute-start(bf16[512,2,1,128]{0,3,2,1:T(8,128)(2,1)} %get-tuple-element.99), channel_id=1, source_target_pairs={{0,24},{8,32},{16,40},{24,48},{32,56},{40,64},{48,72},{56,80},{64,... | collective-permute-start | bytes 786440 | tf_op jit(solution)/shard_map/ppermute | solution.py:22
  95.7 282.8 %collective-permute-start.3 = (bf16[512,2,1,128]{0,3,2,1:T(8,128)(2,1)}, bf16[512,2,1,128]{0,3,2,1:T(8,128)(2,1)}, u32[]{:S(2)}, u32[]{:S(2)}) collective-permute-start(bf16[512,2,1,128]{0,3,2,1:T(8,128)(2,1)} %get-tuple-element.99), channel_id=1, source_target_pairs={{0,32},{8,40},{16,48},{24,56},{32,64},{40,72},{48,80},{56,88},{64,... | collective-permute-start | bytes 786440 | tf_op jit(solution)/shard_map/ppermute | solution.py:22
  110.8 251.9 %copy-start.10 = (bf16[512,1,2,128]{3,0,2,1:T(8,128)(2,1)}, bf16[512,1,2,128]{3,0,2,1:T(8,128)(2,1)S(1)}, u32[]{:S(2)}) copy-start(bf16[512,1,2,128]{3,0,2,1:T(8,128)(2,1)S(1)} %pad_maximum_fusion.1) | copy-start | bytes 786436
  357.9 4.0 copy-start.19
  362.8 4.1 copy-start.18
  368.5 3.7 copy-start.16
  373.2 5.3 %copy-start.3 = (f32[512,1,2,128]{0,3,2,1:T(8,128)}, f32[512,1,2,128]{0,3,2,1:T(8,128)S(1)}, u32[]{:S(2)}) copy-start(f32[512,1,2,128]{0,3,2,1:T(8,128)S(1)} %get-tuple-element.61) | copy-start | bytes 1572868
  380.3 5.7 %copy-start.2 = (f32[512,1,2,128]{0,3,2,1:T(8,128)S(1)}, f32[512,1,2,128]{0,3,2,1:T(8,128)}, u32[]{:S(2)}) copy-start(f32[512,1,2,128]{0,3,2,1:T(8,128)} %copy-done.1) | copy-start | bytes 1572868
  380.3 5.7 %copy-start.4 = (f32[512,1,2,128]{0,3,2,1:T(8,128)S(1)}, f32[512,1,2,128]{0,3,2,1:T(8,128)}, u32[]{:S(2)}) copy-start(f32[512,1,2,128]{0,3,2,1:T(8,128)} %copy-done.3) | copy-start | bytes 1572868
  380.3 5.7 %copy-start.9 = (bf16[2560,2,1,128]{0,3,2,1:T(8,128)(2,1)S(1)}, bf16[2560,2,1,128]{0,3,2,1:T(8,128)(2,1)}, u32[]{:S(2)}) copy-start(bf16[2560,2,1,128]{0,3,2,1:T(8,128)(2,1)} %constant_dynamic-update-slice_fusion) | copy-start | bytes 3932164
  388.5 58.8 %copy-start.6 = (bf16[512,576]{0,1:T(8,128)(2,1)S(1)}, bf16[512,576]{0,1:T(8,128)(2,1)}, u32[]{:S(2)}) copy-start(bf16[512,576]{0,1:T(8,128)(2,1)} %param.20) | copy-start | bytes 1769476
  (3 other events, 2.3 us)
Sparse Core Ops, SparseCore 0:
  10.0 69.4 all-gather.2
  387.8 36.7 all-gather.4
Sparse Core Ops, SparseCore 1:
  15.7 342.2 all-reduce.2
where the time goes:
time: 459 us; the launch traced here: 457 us
  waiting for transfers between devices  338 us (74%)
  matrix products  32.3 us (7%)
  between operations  20.2 us (4%)
  other arithmetic  18.8 us (4%)
  blocking collectives  18.7 us (4%)
  starting transfers between devices  15.1 us (3%)
  local copies, waits for them, and re-layouts  13.4 us (3%)
    psum x1, waiting for transfers between devices, spread(): return lax.psum(jnp.where(mine, array, jnp.zeros_like(array)), axis)  247 us
    all_gather x1, waiting for transfers between devices, on_device(): whole = lax.all_gather(hidden_in, 'tp', axis=1, tiled=True)  54.4 us
    all_gather x1, waiting for transfers between devices, on_device(): lax.all_gather(attended, 'tp', axis=1, tiled=True)  36.1 us
    psum x1, blocking collectives, on_device(): out_sq = lax.psum(jnp.sum(projected * projected, axis=1), 'tp')  18.7 us
    dot_general x4, matrix products, attend(): jnp.einsum('tkgd,skd->tkgs', query_rows, key_rows, preferred_element_type...  17.4 us
    ppermute x4, starting transfers between devices, passed_along(): return lax.ppermute(block, axis, route)  15 us
  transfers between devices with their start and end apart: 7, of which 3 were waited for; matrix products, arithmetic and copies ran while one was open for 10% of the time, Pallas kernels for 0%

commit v1 on v0

v1 whole, which is shorter than its diff:
```python
import math

import jax
import jax.numpy as jnp
import numpy as np
from jax import lax
from jax.experimental import pallas as pl
from jax.experimental.pallas import tpu as pltpu
from jax.sharding import PartitionSpec as P

MESH = pl.DeviceIdType.MESH
WIDTH = 4608
HEAD = 128
QSCALE = 144
PREFIX = 2048
TOK = 512
REQS = 48
SHARD = 576
PIECES = (("P", "R"), ("P", "L"), ("Q", "R"), ("Q", "L"))
SOFTCAP = 50.0
EPS = 1e-6
F32 = jnp.float32
BF16 = jnp.bfloat16


def remote(src, dst, ssem, rsem, where):
    return pltpu.make_async_remote_copy(
        src_ref=src, dst_ref=dst, send_sem=ssem, recv_sem=rsem, device_id=where, device_id_type=MESH
    )


class Gather:
    def __init__(self, own, buf, ssem, rsem, rows, x, l):
        self.own, self.buf, self.ssem, self.rsem, self.rows = own, buf, ssem, rsem, rows
        self.x, self.l = x, l
        self.count = 0
        self.started = []
        self.n = len(PIECES)
        self.prow = rows // self.n

    def target(self, way):
        x, l = self.x, self.l
        if way == "R":
            return {"tp": l * 4 + (x + 1) % 4}
        if way == "L":
            return {"tp": l * 4 + (x + 3) % 4}
        return {"tp": (1 - l) * 4 + x}

    def place(self, dx, dl, k):
        shard = ((self.l + dl) % 2) * 4 + (self.x + dx) % 4
        return self.buf.at[pl.ds(pl.multiple_of(shard * self.rows + k * self.prow, 16), self.prow)]

    def send(self, dx, dl, k, way):
        src = self.place(dx, dl, k)
        if dx == 0 and dl == 0:
            src = self.own.at[pl.ds(k * self.prow, self.prow)]
        rdx, rdl = dx, dl
        if way == "R":
            rdx = (dx + 3) % 4
        elif way == "L":
            rdx = (dx + 1) % 4
        else:
            rdl = 1 - dl
        copy = remote(
            src, self.place(dx, dl, k), self.ssem.at[self.count], self.rsem.at[(rdl * 4 + rdx) * self.n + k], self.target(way)
        )
        copy.start()
        self.count += 1
        self.started.append(copy)

    def wait(self, dx, dl, k):
        here = self.place(dx, dl, k)
        remote(here, here, self.ssem.at[0], self.rsem.at[(dl * 4 + dx) * self.n + k], self.target("R")).wait_recv()

    def start(self):
        for k in range(self.n):
            for way in ("R", "L", "Z"):
                self.send(0, 0, k, way)

    def first(self, k):
        kind, way = PIECES[k]
        self.wait(3, 0, k)
        if way == "R":
            self.send(3, 0, k, "R")
        if kind == "Q":
            self.send(3, 0, k, "Z")
        self.wait(1, 0, k)
        if way == "L":
            self.send(1, 0, k, "L")
        if kind == "Q":
            self.send(1, 0, k, "Z")
        self.wait(0, 1, k)
        if kind == "P":
            self.send(0, 1, k, "R")
            self.send(0, 1, k, "L")

    def second(self, k):
        kind, way = PIECES[k]
        self.wait(2, 0, k)
        if kind == "Q":
            self.send(2, 0, k, "Z")
        self.wait(3, 1, k)
        if kind == "P" and way == "R":
            self.send(3, 1, k, "R")
        self.wait(1, 1, k)
        if kind == "P" and way == "L":
            self.send(1, 1, k, "L")

    def third(self, k):
        self.wait(2, 1, k)

    def drain(self):
        for copy in self.started:
            copy.wait_send()


def gather_sends():
    total = 0
    for kind, _ in PIECES:
        total += 3 + 1 + (3 if kind == "Q" else 3)
    return total


def slot_tables(len_row, order_row, prefix_row):
    a = lax.broadcasted_iota(jnp.int32, (REQS, REQS), 0)
    b = lax.broadcasted_iota(jnp.int32, (REQS, REQS), 1)
    order_col = jnp.sum(jnp.where(a == b, jnp.broadcast_to(order_row, (REQS, REQS)), 0.0), axis=1, keepdims=True)
    chosen = order_col == b.astype(F32)
    length = jnp.sum(jnp.where(chosen, jnp.broadcast_to(len_row, (REQS, REQS)), 0.0), axis=1, keepdims=True)
    prefix = jnp.sum(jnp.where(chosen, jnp.broadcast_to(prefix_row, (REQS, REQS)), 0.0), axis=1, keepdims=True)
    length_row = jnp.sum(jnp.where(a == b, jnp.broadcast_to(length, (REQS, REQS)), 0.0), axis=0, keepdims=True)
    stop = jnp.sum(jnp.where(b <= a, jnp.broadcast_to(length_row, (REQS, REQS)), 0.0), axis=1, keepdims=True)
    return stop - length, stop, prefix


def kernel_in(
    owner_ref, len_ref, order_ref, pref_ref, gain_ref, freq_ref,
    h_hbm, wq_hbm, wk_hbm, wv_hbm, ck_ref, cv_ref,
    q_out, kv_out, f_out,
    h_buf, w_buf, wt, acc, sq, cos_buf, sin_buf, cache_f,
    y0, y1, s0, s1, c0, c1, z0, z1, p0, p1, kv_own,
    g_ssem, g_rsem, y_ssem, y_rsem, b_ssem, b_rsem, z_ssem, z_rsem, t_ssem, t_rsem,
    a_ssem, a_rsem, r_ssem, r_rsem, k_ssem, k_rsem, local_sem,
):
    s = lax.axis_index("seq")
    t = lax.axis_index("tp")
    zh, y, c = s // 8, (s // 2) % 4, s % 2
    l, x = t // 4, t % 4
    other = 1 - c
    sibling = {"seq": zh * 8 + y * 2 + other}

    def at_y(d):
        return {"seq": zh * 8 + ((y + d) % 4) * 2 + c}

    def at_z(d):
        return {"seq": ((zh + d) % 4) * 8 + y * 2 + c}

    ahead = {"seq": (s + 2) % 32}
    behind = {"seq": (s + 30) % 32}
    gather = Gather(h_hbm, h_buf, g_ssem, g_rsem, SHARD, x, l)

    barrier = pltpu.get_barrier_semaphore()
    peers = [gather.target("R"), gather.target("L"), gather.target("Z"), sibling, ahead, behind]
    peers += [at_y(1), at_y(2), at_y(3), at_z(1), at_z(2), at_z(3)]
    for peer in peers:
        pl.semaphore_signal(barrier, inc=1, device_id=peer, device_id_type=MESH)

    local = []

    def copy_here(src, dst):
        cp = pltpu.make_async_copy(src, dst, local_sem.at[len(local)])
        cp.start()
        local.append(cp)
        return cp

    weights = [
        copy_here(wq_hbm, w_buf.at[:, pl.ds(0, 256)]),
        copy_here(wk_hbm, w_buf.at[:, pl.ds(256, 128)]),
        copy_here(wv_hbm, w_buf.at[:, pl.ds(384, 128)]),
        copy_here(h_hbm, h_buf.at[pl.ds(pl.multiple_of(t * SHARD, 16), SHARD)]),
    ]
    pl.semaphore_wait(barrier, len(peers))
    gather.start()

    @pl.loop(0, 16)
    def _(b):
        rows = pl.ds(pl.multiple_of(b * 128, 128), 128)
        cache_f[b, 0:128, :] = ck_ref[rows, :]
        cache_f[b, 128:256, :] = cv_ref[rows, :].astype(F32).T.astype(BF16)

    halves = ((y0, s0, c0, z0, p0), (y1, s1, c1, z1, p1))
    pending = []

    def push(src, dst, ssem, rsem, where):
        cp = remote(src, dst, ssem, rsem, where)
        cp.start()
        pending.append(cp)

    def landed(ref, rsem):
        remote(ref, ref, y_ssem.at[0], rsem, sibling).wait_recv()

    own_y = []
    for h in range(2):
        yb = halves[h][0]
        for d in (1, 3, 2):
            j = (y + d) % 4
            push(cache_f.at[pl.ds(j * 4 + h * 2, 2)], yb.at[y], y_ssem.at[h * 3 + d - 1], y_rsem.at[h * 3 + 3 - d], at_y(d))
        own_y.append(copy_here(cache_f.at[pl.ds(y * 4 + h * 2, 2)], yb.at[y]))

    oc = jnp.int32(-1)
    od = jnp.int32(-1)
    for p in range(4):
        o = owner_ref[p]
        inner = jnp.logical_and(o != 0, o != 31)
        fresh = oc < 0
        od = jnp.where(jnp.logical_and(inner, jnp.logical_not(fresh)), o, od)
        oc = jnp.where(jnp.logical_and(inner, fresh), o, oc)
    oc = jnp.clip(oc, 0, 31)
    od = jnp.clip(od, 0, 31)
    mine = jnp.where(c == 0, oc, od)
    theirs = jnp.where(c == 0, od, oc)

    def quarter(item, j, h):
        return f_out.at[item, pl.ds(j * 4 + h * 2, 2)]

    is_end = zh == 3 * c

    def stage_y(h):
        yb, sb, cb, zb, pb = halves[h]
        own_y[h].wait()
        for d in (1, 3, 2):
            landed(yb.at[(y + d) % 4], y_rsem.at[h * 3 + d - 1])
        sb[...] = yb[(theirs >> 1) & 3]
        push(sb, cb.at[c], b_ssem.at[h], b_rsem.at[h], sibling)

        @pl.when(is_end)
        def _():
            for d in (1, 3, 2):
                remote(yb.at[3 * c], quarter(c, y, h), a_ssem.at[h * 4 + d], a_rsem.at[h], at_z(d)).start()
            pltpu.make_async_copy(yb.at[3 * c], quarter(c, y, h), a_ssem.at[h * 4]).start()

        cb[c] = yb[(mine >> 1) & 3]

    def stage_core(h):
        yb, sb, cb, zb, pb = halves[h]
        landed(cb.at[other], b_rsem.at[h])
        zb[zh] = cb[mine & 1]
        for d in (1, 3, 2):
            push(zb.at[zh], zb.at[zh], z_ssem.at[h * 3 + d - 1], z_rsem.at[h * 3 + 3 - d], at_z(d))

    def relay(item, j, h, i, d):
        n = (i * 4 + d) * 2 + h
        push(quarter(item, j, h), quarter(item, j, h), r_ssem.at[n], r_rsem.at[n], sibling)

    def stage_z(h):
        yb, sb, cb, zb, pb = halves[h]
        for d in (1, 3, 2):
            landed(zb.at[(zh + d) % 4], z_rsem.at[h * 3 + d - 1])

        @pl.when(jnp.logical_not(is_end))
        def _():
            landed(quarter(c, y, h), a_rsem.at[h])

        @pl.when(is_end)
        def _():
            pltpu.make_async_copy(yb.at[3 * c], quarter(c, y, h), a_ssem.at[h * 4]).wait()

        pb[...] = zb[mine >> 3]
        copy_here(pb, quarter(c + 2, y, h))
        for i, src in ((0, quarter(c, y, h)), (1, pb)):
            item = c + 2 * i
            for d in (1, 3):
                push(src, quarter(item, y, h), t_ssem.at[(i * 3 + d - 1) * 2 + h], t_rsem.at[(i * 3 + 3 - d) * 2 + h], at_y(d))
            n = (i * 4) * 2 + h
            push(src, quarter(item, y, h), r_ssem.at[n], r_rsem.at[n], sibling)

    def stage_spread(h):
        for i in range(2):
            item = c + 2 * i
            for d in (3, 1):
                j = (y + d) % 4
                landed(quarter(item, j, h), t_rsem.at[(i * 3 + d - 1) * 2 + h])
                if (i == 0 and d == 3) or (i == 1 and d == 1):
                    push(
                        quarter(item, j, h), quarter(item, j, h), t_ssem.at[(i * 3 + 1) * 2 + h], t_rsem.at[(i * 3 + 1) * 2 + h],
                        at_y(1 if i == 0 else 3),
                    )
                relay(item, j, h, i, d)

    def stage_far(h):
        for i in range(2):
            item = c + 2 * i
            j = (y + 2) % 4
            landed(quarter(item, j, h), t_rsem.at[(i * 3 + 1) * 2 + h])
            relay(item, j, h, i, 2)

    def rotary_tables():
        first, stop, _ = slot_tables(len_ref[...], order_ref[...], pref_ref[...])
        tok = (lax.broadcasted_iota(jnp.int32, (1, TOK), 1) + s * TOK).astype(F32)
        start = jnp.max(jnp.where(stop <= tok, jnp.broadcast_to(stop, (REQS, TOK)), 0.0), axis=0, keepdims=True)
        place = tok - start + float(PREFIX)
        angle = freq_ref[...] * place
        cos_buf[...] = jnp.cos(angle)
        sin_buf[...] = jnp.sin(angle)

    def turn_weights(i):
        @pl.loop(i * 9, i * 9 + 9)
        def _(f):
            rows = pl.ds(pl.multiple_of(f * 128, 128), 128)
            g = gain_ref[pl.ds(f, 1), :]
            for cb in range(4):
                w = w_buf[rows, cb * 128:(cb + 1) * 128].astype(F32).T
                wt[cb * 128:(cb + 1) * 128, rows] = (w * g).astype(BF16)

    def multiply(pair, begin):
        rows = pl.multiple_of(pair * 1152, 128)

        @pl.loop(0, 2)
        def _(m):
            mm = pl.ds(pl.multiple_of(m * 256, 256), 256)
            part = jnp.dot(wt[mm, pl.ds(rows, 1152)], h_buf[pl.ds(rows, 1152), :], preferred_element_type=F32)
            acc[mm, :] = part if begin else acc[mm, :] + part

        @pl.loop(0, 9)
        def _(b):
            v = h_buf[pl.ds(pl.multiple_of(rows + b * 128, 128), 128), :].astype(F32)
            v = v * v
            tot = v[0:8]
            for e in range(1, 16):
                tot = tot + v[e * 8:(e + 1) * 8]
            sq[...] = sq[...] + tot

    sq[...] = jnp.zeros_like(sq)
    for cp in weights:
        cp.wait()
    turn_weights(0)
    gather.first(0)
    stage_y(0)
    stage_core(0)
    turn_weights(1)
    gather.first(1)
    turn_weights(2)
    gather.first(2)
    stage_y(1)
    stage_core(1)
    turn_weights(3)
    gather.first(3)
    near = l * 2 + x // 2
    multiply(near, True)
    rotary_tables()
    gather.second(0)
    stage_z(0)
    gather.second(1)
    gather.second(2)
    gather.second(3)
    multiply(l * 2 + 1 - x // 2, False)
    stage_z(1)
    multiply((1 - l) * 2 + x // 2, False)
    stage_spread(0)
    for k in range(4):
        gather.third(k)
    multiply((1 - l) * 2 + 1 - x // 2, False)

    scale = lax.rsqrt(jnp.sum(sq[...], axis=0, keepdims=True) * (1.0 / WIDTH) + EPS)
    cos, sin = cos_buf[...], sin_buf[...]

    def turned(r0):
        a = acc[r0:r0 + 64, :] * scale
        b = acc[r0 + 64:r0 + 128, :] * scale
        return a * cos - b * sin, b * cos + a * sin

    a, b = turned(256)
    kt = jnp.concatenate([a, b], axis=0)
    vt = (acc[384:512, :] * scale).astype(BF16)
    for blk in range(4):
        kv_own[blk, 0:128, :] = kt[:, blk * 128:(blk + 1) * 128].T.astype(BF16)
        kv_own[blk, 128:256, :] = vt[:, blk * 128:(blk + 1) * 128]

    def kv(slot, g):
        return kv_out.at[slot, pl.ds(g * 2, 2)]

    sib_slot = (5 - 2 * other, 3 - 2 * other, 1 + 4 * other)
    my_slot = (5 - 2 * c, 3 - 2 * c, 1 + 4 * c)
    for g in range(2):
        src = kv_own.at[pl.ds(g * 2, 2)]
        push(src, kv(2, g), k_ssem.at[g], k_rsem.at[g], ahead)
    for g in range(2):
        src = kv_own.at[pl.ds(g * 2, 2)]
        push(src, kv(sib_slot[0], g), k_ssem.at[4 + g], k_rsem.at[4 + g], sibling)
    copy_here(kv_own, kv_out.at[4])
    for hd in range(2):
        a, b = turned(hd * 128)
        q_out[hd * 128:hd * 128 + 64, :] = a.astype(BF16)
        q_out[hd * 128 + 64:hd * 128 + 128, :] = b.astype(BF16)
    stage_spread(1)
    stage_far(0)
    for g in range(2):
        landed(kv(2, g), k_rsem.at[g])
        push(kv(2, g), kv(0, g), k_ssem.at[2 + g], k_rsem.at[2 + g], ahead)
        push(kv(2, g), kv(sib_slot[1], g), k_ssem.at[6 + g], k_rsem.at[6 + g], sibling)
    stage_far(1)
    for g in range(2):
        landed(kv(0, g), k_rsem.at[2 + g])
        push(kv(0, g), kv(sib_slot[2], g), k_ssem.at[8 + g], k_rsem.at[8 + g], sibling)
    for i in range(2):
        item = other + 2 * i
        for d in range(4):
            for h in range(2):
                landed(quarter(item, (y + d) % 4, h), r_rsem.at[(i * 4 + d) * 2 + h])
    for n in range(3):
        for g in range(2):
            landed(kv(my_slot[n], g), k_rsem.at[4 + 2 * n + g])
    gather.drain()
    for cp in pending:
        cp.wait_send()
    for h in range(2):
        @pl.when(is_end)
        def _():
            for d in (1, 3, 2):
                remote(halves[h][0].at[3 * c], quarter(c, y, h), a_ssem.at[h * 4 + d], a_rsem.at[h], at_z(d)).wait_send()
    for cp in local[4 + 2:]:
        cp.wait()


def kernel_attend(
    owner_s, len_s, order_s, pref_s, base_s, len_ref, order_ref, pref_ref, q_ref, kv_hbm, f_hbm,
    out_ref, kv_buf, f_buf, acc, kv_sem, f_sem,
):
    kv_copy = pltpu.make_async_copy(kv_hbm.at[pl.ds(0, 5)], kv_buf, kv_sem)
    kv_copy.start()
    base = base_s[0]
    items = []
    seen = jnp.int32(0)
    for p in range(4):
        o = owner_s[p]
        inner = jnp.logical_and(o != 0, o != 31)
        items.append(jnp.where(o == 0, 0, jnp.where(o == 31, 1, 2 + seen)))
        seen = seen + inner.astype(jnp.int32)

    def look(r, carry):
        at = carry[0]
        req = order_s[r]
        stop = at + len_s[req]
        bit = jnp.int32(1) << pref_s[req]
        out = [stop]
        for rb in range(4):
            lo = base + rb * 128
            hit = jnp.logical_and(at < lo + 128, stop > lo)
            out.append(jnp.where(hit, carry[1 + 2 * rb] | bit, carry[1 + 2 * rb]))
            out.append(jnp.where(jnp.logical_and(at <= lo, stop > lo), at, carry[2 + 2 * rb]))
        return tuple(out)

    zero = jnp.int32(0)
    found = lax.fori_loop(0, REQS, look, (zero,) * 9)
    flags = [found[1 + 2 * rb] for rb in range(4)]
    begins = [found[2 + 2 * rb] for rb in range(4)]
    every = flags[0] | flags[1] | flags[2] | flags[3]
    for p in range(4):
        @pl.when(((every >> p) & 1) == 1)
        def _():
            pltpu.make_async_copy(f_hbm.at[items[p]], f_buf.at[p], f_sem.at[p]).start()

    first, stop, prefix = slot_tables(len_ref[...], order_ref[...], pref_ref[...])
    c1 = float(QSCALE ** -0.5 / SOFTCAP)
    c2 = float(SOFTCAP * math.log2(math.e))
    ones = jnp.ones((16, 256), BF16)
    kv_copy.wait()

    def weigh(k2, qt):
        sc = jnp.dot(k2, qt, preferred_element_type=F32)
        return jnp.exp2(jnp.tanh(sc * c1) * c2)

    for rb in range(4):
        lanes = pl.ds(rb * 128, 128)
        qt = jnp.concatenate([q_ref[0:128, lanes], q_ref[128:256, lanes]], axis=1)
        tok = (lax.broadcasted_iota(jnp.int32, (1, 256), 1) % 128 + (base + rb * 128)).astype(F32)
        begin = jnp.max(jnp.where(stop <= tok, jnp.broadcast_to(stop, (REQS, 256)), 0.0), axis=0, keepdims=True)
        inside = jnp.logical_and(first <= tok, tok < stop)
        pref = jnp.sum(jnp.where(inside, jnp.broadcast_to(prefix, (REQS, 256)), 0.0), axis=0, keepdims=True)
        acc[...] = jnp.zeros_like(acc)
        origin = base - 2048
        low = (begins[rb] - origin) // 256

        @pl.loop(low, (2048 + rb * 128 + 128 + 255) // 256)
        def _(n):
            slot, blk = n // 2, (n % 2) * 2
            k2 = jnp.concatenate([kv_buf[slot, blk, 0:128, :], kv_buf[slot, blk + 1, 0:128, :]], axis=0)
            v2 = jnp.concatenate([kv_buf[slot, blk, 128:256, :], kv_buf[slot, blk + 1, 128:256, :]], axis=1)
            key = (lax.broadcasted_iota(jnp.int32, (256, 1), 0) + (origin + n * 256)).astype(F32)
            ok = jnp.logical_and(key <= tok, key >= begin)
            w = jnp.where(ok, weigh(k2, qt), 0.0).astype(BF16)
            acc[...] += jnp.dot(jnp.concatenate([v2, ones], axis=0), w, preferred_element_type=F32)

        for p in range(4):
            @pl.when(((flags[rb] >> p) & 1) == 1)
            def _():
                @pl.when(((every >> p) & 1) == 1)
                def _():
                    earlier = jnp.int32(0)
                    for q in range(rb):
                        earlier = earlier | flags[q]

                    @pl.when(((earlier >> p) & 1) == 0)
                    def _():
                        pltpu.make_async_copy(f_hbm.at[0], f_buf.at[p], f_sem.at[p]).wait()

                rowmask = pref == float(p)

                @pl.loop(0, 8)
                def _(n):
                    blk = n * 2
                    k2 = jnp.concatenate([f_buf[p, blk, 0:128, :], f_buf[p, blk + 1, 0:128, :]], axis=0)
                    v2 = jnp.concatenate([f_buf[p, blk, 128:256, :], f_buf[p, blk + 1, 128:256, :]], axis=1)
                    w = weigh(k2, qt).astype(BF16)
                    part = jnp.dot(jnp.concatenate([v2, ones], axis=0), w, preferred_element_type=F32)
                    acc[...] += jnp.where(rowmask, part, 0.0)

        att = acc[0:128, :] / acc[128:129, :]
        out_ref[0:128, lanes] = att[:, 0:128].astype(BF16)
        out_ref[128:256, lanes] = att[:, 128:256].astype(BF16)


def kernel_out(
    att_ref, wo_hbm, h_ref, gain_ref, out_ref, g_buf, wo_buf, acc, gcol, sums, g_ssem, g_rsem, q_ssem, q_rsem, local_sem
):
    s = lax.axis_index("seq")
    t = lax.axis_index("tp")
    l, x = t // 4, t % 4
    gather = Gather(att_ref, g_buf, g_ssem, g_rsem, 256, x, l)

    def peer(d):
        return {"tp": (t + d) % 8}

    barrier = pltpu.get_barrier_semaphore()
    for d in range(1, 8):
        pl.semaphore_signal(barrier, inc=1, device_id=peer(d), device_id_type=MESH)
    wo_copy = pltpu.make_async_copy(wo_hbm, wo_buf, local_sem.at[0])
    own_copy = pltpu.make_async_copy(att_ref, g_buf.at[pl.ds(pl.multiple_of(t * 256, 256), 256)], local_sem.at[1])
    wo_copy.start()
    own_copy.start()
    pl.semaphore_wait(barrier, 7)
    gather.start()

    g5 = gain_ref[t]
    for b in range(5):
        gcol[b * 128:(b + 1) * 128, :] = jnp.broadcast_to(g5[b:b + 1, :], (128, 128)).T
    wo_copy.wait()
    own_copy.wait()

    def multiply(dx, dl, begin):
        shard = ((l + dl) % 2) * 4 + (x + dx) % 4
        rows = pl.ds(pl.multiple_of(shard * 256, 256), 256)

        @pl.loop(0, 4)
        def _(m):
            mm = pl.ds(pl.multiple_of(m * 144, 16), 144)
            part = jnp.dot(wo_buf[mm, rows], g_buf[rows, :], preferred_element_type=F32)
            acc[mm, :] = part if begin else acc[mm, :] + part

    multiply(0, 0, True)
    for k in range(4):
        gather.first(k)
    multiply(1, 0, False)
    multiply(3, 0, False)
    multiply(0, 1, False)
    for k in range(4):
        gather.second(k)
    multiply(2, 0, False)
    multiply(1, 1, False)
    multiply(3, 1, False)
    for k in range(4):
        gather.third(k)
    multiply(2, 1, False)

    tot = jnp.zeros((8, TOK), F32)
    for b in range(72):
        v = acc[b * 8:(b + 1) * 8, :]
        tot = tot + v * v
    sums[t] = tot
    copies = []
    for d in range(1, 8):
        cp = remote(sums.at[t], sums.at[t], q_ssem.at[d - 1], q_rsem.at[7 - d], peer(d))
        cp.start()
        copies.append(cp)
    for d in range(1, 8):
        here = sums.at[(t + d) % 8]
        remote(here, here, q_ssem.at[0], q_rsem.at[d - 1], peer(1)).wait_recv()
    tot = sums[0]
    for d in range(1, 8):
        tot = tot + sums[d]
    scale = lax.rsqrt(jnp.sum(tot, axis=0, keepdims=True) * (1.0 / WIDTH) + EPS)
    for b in range(9):
        rows = slice(b * 64, b * 64 + 64)
        g = gcol[rows, :]
        for n in range(4):
            cols = slice(n * 128, n * 128 + 128)
            post = acc[rows, cols] * scale[:, cols] * g
            out_ref[rows, cols] = (h_ref[rows, cols].astype(F32) + post).astype(BF16)
    gather.drain()
    for cp in copies:
        cp.wait_send()


def on_device(
    hidden_in, pre_gain, post_gain, w_query, key_weight, value_weight, w_out, cache, suffix_len, request_order,
    request_prefix, prefix_owner,
):
    any_spec = pl.BlockSpec(memory_space=pl.ANY)
    vmem = pl.BlockSpec(memory_space=pltpu.VMEM)
    smem = pl.BlockSpec(memory_space=pltpu.SMEM)
    dma = pltpu.SemaphoreType.DMA
    h_t = hidden_in.T
    len_row = suffix_len.astype(F32).reshape(1, REQS)
    order_row = request_order.astype(F32).reshape(1, REQS)
    pref_row = request_prefix.astype(F32).reshape(1, REQS)
    freq = jnp.asarray((10000.0 ** (-2.0 * np.arange(64) / HEAD)).astype(np.float32).reshape(64, 1))
    sends = gather_sends()
    n = len(PIECES)
    half = pltpu.VMEM((2, 256, 128), BF16)
    four = pltpu.VMEM((4, 2, 256, 128), BF16)
    two = pltpu.VMEM((2, 2, 256, 128), BF16)
    q, kv, spread = pl.pallas_call(
        kernel_in,
        out_shape=(
            jax.ShapeDtypeStruct((256, TOK), BF16),
            jax.ShapeDtypeStruct((6, 4, 256, 128), BF16),
            jax.ShapeDtypeStruct((4, 16, 256, 128), BF16),
        ),
        in_specs=[smem, vmem, vmem, vmem, vmem, vmem, any_spec, any_spec, any_spec, any_spec, vmem, vmem],
        out_specs=(vmem, any_spec, any_spec),
        scratch_shapes=[
            pltpu.VMEM((WIDTH, TOK), BF16),
            pltpu.VMEM((WIDTH, 512), BF16),
            pltpu.VMEM((512, WIDTH), BF16),
            pltpu.VMEM((512, TOK), F32),
            pltpu.VMEM((8, TOK), F32),
            pltpu.VMEM((64, TOK), F32),
            pltpu.VMEM((64, TOK), F32),
            pltpu.VMEM((16, 256, 128), BF16),
            four, four, half, half, two, two, four, four, half, half,
            pltpu.VMEM((4, 256, 128), BF16),
            dma((sends,)), dma((8 * n,)), dma((6,)), dma((6,)), dma((2,)), dma((2,)), dma((6,)), dma((6,)),
            dma((12,)), dma((12,)), dma((8,)), dma((2,)), dma((16,)), dma((16,)), dma((10,)), dma((10,)), dma((12,)),
        ],
        compiler_params=pltpu.CompilerParams(collective_id=0, has_side_effects=True, vmem_limit_bytes=60 << 20),
    )(
        prefix_owner, len_row, order_row, pref_row, pre_gain.reshape(36, 128), freq,
        h_t, w_query, key_weight, value_weight, cache[:, 0, :], cache[:, 1, :],
    )
    base = (lax.axis_index("seq") * TOK).astype(jnp.int32).reshape(1)
    att = pl.pallas_call(
        kernel_attend,
        out_shape=jax.ShapeDtypeStruct((256, TOK), BF16),
        in_specs=[smem] * 5 + [vmem] * 4 + [any_spec, any_spec],
        out_specs=vmem,
        scratch_shapes=[
            pltpu.VMEM((5, 4, 256, 128), BF16),
            pltpu.VMEM((4, 16, 256, 128), BF16),
            pltpu.VMEM((144, 256), F32),
            dma, dma((4,)),
        ],
        compiler_params=pltpu.CompilerParams(vmem_limit_bytes=32 << 20),
    )(prefix_owner, suffix_len, request_order, request_prefix, base, len_row, order_row, pref_row, q, kv, spread)
    gains = jnp.pad(post_gain.reshape(8, SHARD), ((0, 0), (0, 64))).reshape(8, 5, 128)
    out = pl.pallas_call(
        kernel_out,
        out_shape=jax.ShapeDtypeStruct((SHARD, TOK), BF16),
        in_specs=[vmem, any_spec, vmem, vmem],
        out_specs=vmem,
        scratch_shapes=[
            pltpu.VMEM((2048, TOK), BF16),
            pltpu.VMEM((SHARD, 2048), BF16),
            pltpu.VMEM((SHARD, TOK), F32),
            pltpu.VMEM((640, 128), F32),
            pltpu.VMEM((8, 8, TOK), F32),
            dma((sends,)), dma((8 * n,)), dma((7,)), dma((7,)), dma((2,)),
        ],
        compiler_params=pltpu.CompilerParams(collective_id=1, has_side_effects=True, vmem_limit_bytes=32 << 20),
    )(att, w_out.T, h_t, gains)
    return out.T


def solution(mesh):
    placed = (
        P("seq", "tp"), P(), P(), P(None, "tp"), P(None, "tp"), P(None, "tp"), P(None, "tp"), P("seq", None, "tp"),
        P(), P(), P(), P(),
    )
    return jax.shard_map(on_device, mesh=mesh, in_specs=placed, out_specs=P("seq", "tp"), check_vma=False)
```

time: 459 us -> 173 us (0.38)
  the two profiles are of different devices: /device:TPU:2 before, /device:TPU:73 now
where the time goes in v1:
time: 173 us
  Pallas kernels  162 us (94%)
  local copies, waits for them, and re-layouts  9.95 us (6%)
    pallas_call x1, Pallas kernels, on_device(): pl.pallas_call(kernel_in, out_shape=(jax.ShapeDtypeStruct((256, TOK), BF1...  104 us
    pallas_call x1, Pallas kernels, on_device(): pl.pallas_call(kernel_out, out_shape=jax.ShapeDtypeStruct((SHARD, TOK), B...  29.5 us
    pallas_call x1, Pallas kernels, on_device(): pl.pallas_call(kernel_attend, out_shape=jax.ShapeDtypeStruct((256, TOK),...  28 us
    unnamed x27, local copies, waits for them, and re-layouts  5.4 us

profile of v1, /device:TPU:73, one launch (start us, length us, event | category | flops | bytes accessed | tf_op | source)
XLA Modules:
  0.0 172.7 jit_solution(5822121206197121280)
XLA Ops:
  0.0 3.3 %fusion = (bf16[2048,1,128]{2,1,0:T(2,128)(2,1)S(1)}, bf16[2048,1,128]{2,1,0:T(2,128)(2,1)S(1)}) fusion(bf16[2048,2,128]{2,1,0:T(2,128)(2,1)} %param.20), kind=kLoop, calls=%fused_computation.6 | loop fusion | bytes 2097152 | tf_op jit(solution)/shard_map/slice | solution.py:648
  3.3 0.0 copy-start.9
  3.4 0.0 copy-start.10
  3.4 0.0 copy-start.11
  3.4 1.1 copy_bitcast_fusion
  4.5 0.0 copy-done.9
  4.5 0.0 copy-done.10
  4.5 0.6 convert_bitcast_fusion
  5.1 0.0 copy-done.11
  5.1 0.5 convert_bitcast_fusion.2.len_ref
  5.6 104.0 %shard_map.127 = (bf16[256,512]{1,0:T(8,128)(2,1)}, bf16[6,4,256,128]{3,2,1,0:T(8,128)(2,1)}, bf16[4,16,256,128]{3,2,1,0:T(8,128)(2,1)}) custom-call(s32[4]{0:T(128)} %owner_s.1, f32[1,48]{1,0:T(1,128)} %convert_bitcast_fusion.2.len_ref, f32[1,48]{1,0:T(1,128)} %get-tuple-element.16.order_ref, f32[1,48]{1,0:T(1,128)} %get-tuple-element.15.pref_ref, ...), custom_call_target="tpu_custom_call" | custom-call | tf_op jit(solution)/shard_map/pallas_call | solution.py:622
  109.6 0.0 copy-done.5
  109.6 0.0 copy-done.6
  109.6 0.0 copy-done.7
  109.7 0.0 copy-done.8
  109.7 0.0 copy-start
  109.7 2.2 %copy-done = bf16[4,16,256,128]{3,2,1,0:T(8,128)(2,1)S(1)} copy-done((bf16[4,16,256,128]{3,2,1,0:T(8,128)(2,1)S(1)}, bf16[4,16,256,128]{3,2,1,0:T(8,128)(2,1)}, u32[]{:S(2)}) %copy-start) | copy-done | bytes 4194328
  111.9 1.4 copy-done.3
  113.3 0.9 copy-done.4
  114.2 28.0 %shard_map.128.att_ref = bf16[256,512]{1,0:T(8,128)(2,1)S(1)} custom-call(s32[4]{0:T(128)S(1)} %copy-done.7, s32[48]{0:T(128)S(1)} %copy-done.11, s32[48]{0:T(128)S(1)} %copy-done.9, s32[48]{0:T(128)S(1)} %copy-done.10, s32[1]{0:T(128)} %bitcast.base_s, f32[1,48]{1,0:T(1,128)S(1)} %copy-done.8, f32[1,48]{1,0:T(1,128)S(1)} %copy-done.6, ...), custom_call_target="tpu_custom_call" | custom-call | tf_op jit(solution)/shard_map/pallas_call | solution.py:651
  142.2 0.0 copy-done.12
  142.2 0.1 reshape.26
  142.4 29.5 %shard_map.129 = bf16[576,512]{1,0:T(8,128)(2,1)S(1)} custom-call(bf16[256,512]{1,0:T(8,128)(2,1)S(1)} %shard_map.128.att_ref, bf16[576,2048]{1,0:T(8,128)(2,1)S(1)} %bitcast.19, bf16[576,512]{1,0:T(8,128)(2,1)S(1)} %bitcast.18, f32[8,5,128]{2,1,0:T(8,128)S(1)} %copy.18.gain_ref), custom_call_target="tpu_custom_call" | custom-call | tf_op jit(solution)/shard_map/pallas_call | solution.py:665
  171.9 0.8 copy.24
  (13 shorter events, 0.0 us)
Async XLA Ops:
  3.3 1.2 copy-start.9
  3.4 1.2 copy-start.10
  3.4 1.7 copy-start.11
  5.6 104.0 %copy-start.5 = (f32[1,48]{1,0:T(1,128)S(1)}, f32[1,48]{1,0:T(1,128)}, u32[]{:S(2)}) copy-start(f32[1,48]{1,0:T(1,128)} %get-tuple-element.15.pref_ref) | copy-start | bytes 580
  5.6 104.0 %copy-start.6 = (f32[1,48]{1,0:T(1,128)S(1)}, f32[1,48]{1,0:T(1,128)}, u32[]{:S(2)}) copy-start(f32[1,48]{1,0:T(1,128)} %get-tuple-element.16.order_ref) | copy-start | bytes 580
  5.6 104.0 %copy-start.7 = (s32[4]{0:T(128)S(1)}, s32[4]{0:T(128)}, u32[]{:S(2)}) copy-start(s32[4]{0:T(128)} %owner_s.1) | copy-start | bytes 52
  5.6 104.0 %copy-start.8 = (f32[1,48]{1,0:T(1,128)S(1)}, f32[1,48]{1,0:T(1,128)}, u32[]{:S(2)}) copy-start(f32[1,48]{1,0:T(1,128)} %convert_bitcast_fusion.2.len_ref) | copy-start | bytes 580
  109.7 2.2 %copy-start = (bf16[4,16,256,128]{3,2,1,0:T(8,128)(2,1)S(1)}, bf16[4,16,256,128]{3,2,1,0:T(8,128)(2,1)}, u32[]{:S(2)}) copy-start(bf16[4,16,256,128]{3,2,1,0:T(8,128)(2,1)} %get-tuple-element.10.f_hbm) | copy-start | bytes 12582916
  111.9 1.4 copy-start.3
  113.3 0.9 copy-start.4
  114.2 28.0 %copy-start.12 = (f32[4608]{0:T(1024)S(1)}, f32[4608]{0:T(1024)}, u32[]{:S(2)}) copy-start(f32[4608]{0:T(1024)} %param.15) | copy-start | bytes 55300
  114.2 28.1 %copy-start.1 = (bf16[512,576]{0,1:T(8,128)(2,1)S(1)}, bf16[512,576]{0,1:T(8,128)(2,1)}, u32[]{:S(2)}) copy-start(bf16[512,576]{0,1:T(8,128)(2,1)} %param.13) | copy-start | bytes 1769476
  114.2 28.1 %copy-start.2 = (bf16[2048,576]{0,1:T(8,128)(2,1)S(1)}, bf16[2048,576]{0,1:T(8,128)(2,1)}, u32[]{:S(2)}) copy-start(bf16[2048,576]{0,1:T(8,128)(2,1)} %param.19) | copy-start | bytes 7077892

commit v2 on v1

v2 whole, which is shorter than its diff:
```python
import math

import jax
import jax.numpy as jnp
import numpy as np
from jax import lax
from jax.experimental import pallas as pl
from jax.experimental.pallas import tpu as pltpu
from jax.sharding import PartitionSpec as P

MESH = pl.DeviceIdType.MESH
WIDTH = 4608
HEAD = 128
QSCALE = 144
PREFIX = 2048
TOK = 512
REQS = 48
SHARD = 576
IN_PIECES = (("P", "R"), ("P", "L"), ("P", "R"), ("P", "L"))
OUT_PIECES = (("P", "R"), ("P", "L"), ("Q", "R"), ("Q", "L"))
SOFTCAP = 50.0
EPS = 1e-6
KEYS = 512
ON = ("mm", "gather", "prefix", "kv")
SCHED = (
    ("W", 0), ("g1", 0), ("sy", 0), ("sc", 0), ("W", 1), ("g1", 1), ("sr", 0), ("W", 2), ("g1", 2),
    ("so", 0), ("sy", 1), ("sc", 1), ("W", 3), ("g1", 3), ("ss", 0), ("sr", 1), ("M", 0), ("rot", 0),
    ("g2", 0), ("se", 0), ("sz", 0), ("so", 1), ("g2", 1), ("g2", 2), ("ss", 1), ("sp", 0), ("g2", 3),
    ("M", 1), ("se", 1), ("sz", 1), ("M", 2), ("sf", 0), ("g3", 0), ("g3", 1), ("g3", 2), ("g3", 3),
    ("M", 3), ("fin", 0), ("kv", 0), ("q", 0), ("sp", 1), ("kt", 0), ("kt", 1), ("k1", 0), ("k1", 1),
    ("sf", 1), ("k2", 0), ("k2", 1),
)
F32 = jnp.float32
BF16 = jnp.bfloat16


def remote(src, dst, ssem, rsem, where):
    return pltpu.make_async_remote_copy(
        src_ref=src, dst_ref=dst, send_sem=ssem, recv_sem=rsem, device_id=where, device_id_type=MESH
    )


class Gather:
    def __init__(self, pieces, own, buf, ssem, rsem, rows, x, l):
        self.pieces = pieces
        self.own, self.buf, self.ssem, self.rsem, self.rows = own, buf, ssem, rsem, rows
        self.x, self.l = x, l
        self.count = 0
        self.started = []
        self.n = len(pieces)
        self.prow = rows // self.n

    def target(self, way):
        x, l = self.x, self.l
        if way == "R":
            return {"tp": l * 4 + (x + 1) % 4}
        if way == "L":
            return {"tp": l * 4 + (x + 3) % 4}
        return {"tp": (1 - l) * 4 + x}

    def place(self, dx, dl, k):
        shard = ((self.l + dl) % 2) * 4 + (self.x + dx) % 4
        return self.buf.at[pl.ds(pl.multiple_of(shard * self.rows + k * self.prow, 16), self.prow)]

    def send(self, dx, dl, k, way):
        src = self.place(dx, dl, k)
        if dx == 0 and dl == 0:
            src = self.own.at[pl.ds(k * self.prow, self.prow)]
        rdx, rdl = dx, dl
        if way == "R":
            rdx = (dx + 3) % 4
        elif way == "L":
            rdx = (dx + 1) % 4
        else:
            rdl = 1 - dl
        copy = remote(
            src, self.place(dx, dl, k), self.ssem.at[self.count], self.rsem.at[(rdl * 4 + rdx) * self.n + k], self.target(way)
        )
        copy.start()
        self.count += 1
        self.started.append(copy)

    def wait(self, dx, dl, k):
        here = self.place(dx, dl, k)
        remote(here, here, self.ssem.at[0], self.rsem.at[(dl * 4 + dx) * self.n + k], self.target("R")).wait_recv()

    def start(self):
        for k in range(self.n):
            for way in ("R", "L", "Z"):
                self.send(0, 0, k, way)

    def first(self, k):
        kind, way = self.pieces[k]
        self.wait(3, 0, k)
        if way == "R":
            self.send(3, 0, k, "R")
        if kind == "Q":
            self.send(3, 0, k, "Z")
        self.wait(1, 0, k)
        if way == "L":
            self.send(1, 0, k, "L")
        if kind == "Q":
            self.send(1, 0, k, "Z")
        self.wait(0, 1, k)
        if kind == "P":
            self.send(0, 1, k, "R")
            self.send(0, 1, k, "L")

    def second(self, k):
        kind, way = self.pieces[k]
        self.wait(2, 0, k)
        if kind == "Q":
            self.send(2, 0, k, "Z")
        self.wait(3, 1, k)
        if kind == "P" and way == "R":
            self.send(3, 1, k, "R")
        self.wait(1, 1, k)
        if kind == "P" and way == "L":
            self.send(1, 1, k, "L")

    def third(self, k):
        self.wait(2, 1, k)

    def drain(self):
        for copy in self.started:
            copy.wait_send()


def slot_tables(len_row, order_row, prefix_row):
    len_row, order_row, prefix_row = (v.astype(F32) for v in (len_row, order_row, prefix_row))
    a = lax.broadcasted_iota(jnp.int32, (REQS, REQS), 0)
    b = lax.broadcasted_iota(jnp.int32, (REQS, REQS), 1)
    order_col = jnp.sum(jnp.where(a == b, jnp.broadcast_to(order_row, (REQS, REQS)), 0.0), axis=1, keepdims=True)
    chosen = order_col == b.astype(F32)
    length = jnp.sum(jnp.where(chosen, jnp.broadcast_to(len_row, (REQS, REQS)), 0.0), axis=1, keepdims=True)
    prefix = jnp.sum(jnp.where(chosen, jnp.broadcast_to(prefix_row, (REQS, REQS)), 0.0), axis=1, keepdims=True)
    length_row = jnp.sum(jnp.where(a == b, jnp.broadcast_to(length, (REQS, REQS)), 0.0), axis=0, keepdims=True)
    stop = jnp.sum(jnp.where(b <= a, jnp.broadcast_to(length_row, (REQS, REQS)), 0.0), axis=1, keepdims=True)
    return stop - length, stop, prefix


def kernel_in(
    owner_ref, len_ref, order_ref, pref_ref, gain_ref, freq_ref,
    h_hbm, wq_hbm, wk_hbm, wv_hbm, cache_ref,
    q_out, kv_out, f_out,
    h_buf, w_buf, wt, acc, sq, cos_buf, sin_buf, cache_f,
    y0, y1, s0, s1, c0, c1, z0, z1, p0, p1, i0, i1, m0, m1, kv_own, kv_via,
    g_ssem, g_rsem, y_ssem, y_rsem, b_ssem, b_rsem, z_ssem, z_rsem, t_ssem, t_rsem,
    a_ssem, a_rsem, e_sem, r_ssem, r_rsem, k_ssem, k_rsem, local_sem,
):
    s = lax.axis_index("seq")
    t = lax.axis_index("tp")
    zh, y, c = s // 8, (s // 2) % 4, s % 2
    l, x = t // 4, t % 4
    other = 1 - c
    sibling = {"seq": zh * 8 + y * 2 + other}

    def at_y(d):
        return {"seq": zh * 8 + ((y + d) % 4) * 2 + c}

    def at_z(d):
        return {"seq": ((zh + d) % 4) * 8 + y * 2 + c}

    gather = Gather(IN_PIECES, h_hbm, h_buf, g_ssem, g_rsem, SHARD, x, l)

    barrier = pltpu.get_barrier_semaphore()
    peers = [gather.target("R"), gather.target("L"), gather.target("Z"), sibling]
    peers += [at_y(1), at_y(2), at_y(3), at_z(1), at_z(3)]
    for peer in peers:
        pl.semaphore_signal(barrier, inc=1, device_id=peer, device_id_type=MESH)

    local = []

    def copy_here(src, dst):
        cp = pltpu.make_async_copy(src, dst, local_sem.at[len(local)])
        cp.start()
        local.append(cp)
        return cp

    weights = [
        copy_here(wq_hbm, w_buf.at[:, pl.ds(0, 256)]),
        copy_here(wk_hbm, w_buf.at[:, pl.ds(256, 128)]),
        copy_here(wv_hbm, w_buf.at[:, pl.ds(384, 128)]),
        copy_here(h_hbm, h_buf.at[pl.ds(pl.multiple_of(t * SHARD, 16), SHARD)]),
    ]
    pl.semaphore_wait(barrier, len(peers))
    if "gather" in ON:
        gather.start()

    to = lax.broadcasted_iota(jnp.int32, (256, 256), 0)
    of = lax.broadcasted_iota(jnp.int32, (256, 256), 1)
    apart = jnp.where(of == 2 * to - jnp.where(to < 128, 0, 255), 1.0, 0.0).astype(BF16)

    def split_cache(b0, b1):
        @pl.loop(b0, b1)
        def _(b):
            rows = pl.ds(pl.multiple_of(b * 256, 256), 256)
            both = jnp.dot(apart, cache_ref[rows, :], preferred_element_type=F32)
            cache_f[b * 2] = both[0:128].astype(BF16)
            cache_f[b * 2 + 1] = both[128:256].T.astype(BF16)

    if "prefix" in ON:
        split_cache(0, 16)

    halves = ((y0, s0, c0, z0, p0), (y1, s1, c1, z1, p1))
    zin, zmid = (i0, i1), (m0, m1)
    pending = []

    def push(src, dst, ssem, rsem, where):
        cp = remote(src, dst, ssem, rsem, where)
        cp.start()
        pending.append(cp)

    def landed(ref, rsem):
        remote(ref, ref, y_ssem.at[0], rsem, sibling).wait_recv()

    own_y = []
    for h in (range(2) if "prefix" in ON else ()):
        yb = halves[h][0]
        for d in (1, 3, 2):
            j = (y + d) % 4
            push(cache_f.at[pl.ds(j * 8 + h * 4, 4)], yb.at[y], y_ssem.at[h * 3 + d - 1], y_rsem.at[h * 3 + 3 - d], at_y(d))
        own_y.append(copy_here(cache_f.at[pl.ds(y * 8 + h * 4, 4)], yb.at[y]))

    oc = jnp.int32(-1)
    od = jnp.int32(-1)
    for p in range(4):
        o = owner_ref[p]
        inner = jnp.logical_and(o != 0, o != 31)
        fresh = oc < 0
        od = jnp.where(jnp.logical_and(inner, jnp.logical_not(fresh)), o, od)
        oc = jnp.where(jnp.logical_and(inner, fresh), o, oc)
    oc = jnp.clip(oc, 0, 31)
    od = jnp.clip(od, 0, 31)
    mine = jnp.where(c == 0, oc, od)
    theirs = jnp.where(c == 0, od, oc)

    def quarter(item, j, h):
        return f_out.at[item, pl.ds(j * 8 + h * 4, 4)]

    far = (zh - 3 * c) % 4

    def end_copy(h, d, src):
        return remote(src, quarter(c, y, h), a_ssem.at[h * 2 + d // 2], a_rsem.at[h], at_z(d))

    def stage_y(h):
        yb, sb, cb, zb, pb = halves[h]
        own_y[h].wait()
        for d in (1, 3, 2):
            landed(yb.at[(y + d) % 4], y_rsem.at[h * 3 + d - 1])
        sb[...] = yb[(theirs >> 1) & 3]
        push(sb, cb.at[c], b_ssem.at[h], b_rsem.at[h], sibling)

        @pl.when(far == 0)
        def _():
            end_copy(h, 1, yb.at[3 * c]).start()
            end_copy(h, 3, yb.at[3 * c]).start()
            pltpu.make_async_copy(yb.at[3 * c], quarter(c, y, h), e_sem.at[h]).start()

        cb[c] = yb[(mine >> 1) & 3]

    def unit(ref, d):
        return ref.at[(zh + 4 - d) % 4]

    def zsem(sem, h, n):
        return sem.at[h * 6 + n]

    def stage_core(h):
        yb, sb, cb, zb, pb = halves[h]
        landed(cb.at[other], b_rsem.at[h])
        zb[...] = cb[mine & 1]
        push(unit(zb, 2), zin[h].at[0], zsem(z_ssem, h, 0), zsem(z_rsem, h, 0), at_z(3))
        push(unit(zb, 3), zin[h].at[1], zsem(z_ssem, h, 1), zsem(z_rsem, h, 1), at_z(1))

    zo = mine >> 3

    def stage_reduce(h):
        yb, sb, cb, zb, pb = halves[h]
        landed(zin[h].at[0], zsem(z_rsem, h, 0))
        zmid[h][...] = jnp.where(zo == (zh + 1) % 4, zin[h][0], zb[(zh + 3) % 4])
        push(zmid[h], zin[h].at[2], zsem(z_ssem, h, 2), zsem(z_rsem, h, 2), at_z(3))

        @pl.when(jnp.logical_or(far == 1, far == 3))
        def _():
            landed(quarter(c, y, h), a_rsem.at[h])

        @pl.when(far == (1 if h == 0 else 3))
        def _():
            end_copy(h, 1 if h == 0 else 3, quarter(c, y, h)).start()

    def stage_root(h):
        yb, sb, cb, zb, pb = halves[h]
        landed(zin[h].at[1], zsem(z_rsem, h, 1))
        landed(zin[h].at[2], zsem(z_rsem, h, 2))
        whole = jnp.where(zo == zh, zb[zh], jnp.where(zo == (zh + 3) % 4, zin[h][1], zin[h][2]))
        pb[zh] = whole
        push(unit(pb, 0), unit(pb, 0), zsem(z_ssem, h, 3), zsem(z_rsem, h, 3), at_z(1))
        push(unit(pb, 0), unit(pb, 0), zsem(z_ssem, h, 4), zsem(z_rsem, h, 4), at_z(3))

    def relay(item, j, h, i, d):
        n = (i * 4 + d) * 2 + h
        push(quarter(item, j, h), quarter(item, j, h), r_ssem.at[n], r_rsem.at[n], sibling)

    def stage_pass(h):
        yb, sb, cb, zb, pb = halves[h]
        landed(unit(pb, 1), zsem(z_rsem, h, 3))
        push(unit(pb, 1), unit(pb, 1), zsem(z_ssem, h, 5), zsem(z_rsem, h, 5), at_z(1))

    def spread_own(h, i, src):
        item = c + 2 * i
        for d in (1, 3):
            push(src, quarter(item, y, h), t_ssem.at[(i * 3 + d - 1) * 2 + h], t_rsem.at[(i * 3 + 3 - d) * 2 + h], at_y(d))
        n = (i * 4) * 2 + h
        push(src, quarter(item, y, h), r_ssem.at[n], r_rsem.at[n], sibling)

    def stage_end(h):
        yb, sb, cb, zb, pb = halves[h]

        @pl.when(far == 2)
        def _():
            landed(quarter(c, y, h), a_rsem.at[h])

        @pl.when(far == 0)
        def _():
            pltpu.make_async_copy(yb.at[3 * c], quarter(c, y, h), e_sem.at[h]).wait()

        spread_own(h, 0, quarter(c, y, h))

    def stage_z(h):
        yb, sb, cb, zb, pb = halves[h]
        landed(unit(pb, 3), zsem(z_rsem, h, 4))
        landed(unit(pb, 2), zsem(z_rsem, h, 5))
        copy_here(pb, quarter(c + 2, y, h))
        spread_own(h, 1, pb)

    def end_drain(h):
        @pl.when(far == 0)
        def _():
            end_copy(h, 1, quarter(c, y, h)).wait_send()
            end_copy(h, 3, quarter(c, y, h)).wait_send()

        @pl.when(far == (1 if h == 0 else 3))
        def _():
            end_copy(h, 1 if h == 0 else 3, quarter(c, y, h)).wait_send()

    def stage_spread(h):
        for i in range(2):
            item = c + 2 * i
            for d in (3, 1):
                j = (y + d) % 4
                landed(quarter(item, j, h), t_rsem.at[(i * 3 + d - 1) * 2 + h])
                if (i == 0 and d == 3) or (i == 1 and d == 1):
                    push(
                        quarter(item, j, h), quarter(item, j, h), t_ssem.at[(i * 3 + 1) * 2 + h], t_rsem.at[(i * 3 + 1) * 2 + h],
                        at_y(1 if i == 0 else 3),
                    )
                relay(item, j, h, i, d)

    def stage_far(h):
        for i in range(2):
            item = c + 2 * i
            j = (y + 2) % 4
            landed(quarter(item, j, h), t_rsem.at[(i * 3 + 1) * 2 + h])
            relay(item, j, h, i, 2)

    def rotary_tables():
        first, stop, _ = slot_tables(len_ref[...], order_ref[...], pref_ref[...])
        tok = (lax.broadcasted_iota(jnp.int32, (1, TOK), 1) + s * TOK).astype(F32)
        start = jnp.max(jnp.where(stop <= tok, jnp.broadcast_to(stop, (REQS, TOK)), 0.0), axis=0, keepdims=True)
        place = tok - start + float(PREFIX)
        angle = freq_ref[...] * place
        cos_buf[...] = jnp.cos(angle)
        sin_buf[...] = jnp.sin(angle)

    def turn_weights(i):
        @pl.loop(i * 9, i * 9 + 9)
        def _(f):
            rows = pl.ds(pl.multiple_of(f * 128, 128), 128)
            g = gain_ref[pl.ds(f, 1), :]
            for cb in range(4):
                w = w_buf[rows, cb * 128:(cb + 1) * 128].astype(F32).T
                wt[cb * 128:(cb + 1) * 128, rows] = (w * g).astype(BF16)

    def multiply(pair, begin):
        rows = pl.multiple_of(pair * 1152, 128)

        @pl.loop(0, 2)
        def _(m):
            mm = pl.ds(pl.multiple_of(m * 256, 256), 256)
            part = jnp.dot(wt[mm, pl.ds(rows, 1152)], h_buf[pl.ds(rows, 1152), :], preferred_element_type=F32)
            acc[mm, :] = part if begin else acc[mm, :] + part

        @pl.loop(0, 9)
        def _(b):
            v = h_buf[pl.ds(pl.multiple_of(rows + b * 128, 128), 128), :].astype(F32)
            v = v * v
            tot = v[0:8]
            for e in range(1, 16):
                tot = tot + v[e * 8:(e + 1) * 8]
            sq[...] = sq[...] + tot

    sq[...] = jnp.zeros_like(sq)
    for cp in weights:
        cp.wait()

    def finish():
        scale = lax.rsqrt(jnp.sum(sq[...], axis=0, keepdims=True) * (1.0 / WIDTH) + EPS)
        cos, sin = cos_buf[...], sin_buf[...]

        def turned(r0):
            a = acc[r0:r0 + 64, :] * scale
            b = acc[r0 + 64:r0 + 128, :] * scale
            return a * cos - b * sin, b * cos + a * sin

        a, b = turned(256)
        kt = jnp.concatenate([a, b], axis=0)
        vt = (acc[384:512, :] * scale).astype(BF16)
        for blk in range(4):
            kv_own[blk, 0:128, :] = kt[:, blk * 128:(blk + 1) * 128].T.astype(BF16)
            kv_own[blk, 128:256, :] = vt[:, blk * 128:(blk + 1) * 128]

    def queries():
        scale = lax.rsqrt(jnp.sum(sq[...], axis=0, keepdims=True) * (1.0 / WIDTH) + EPS)
        cos, sin = cos_buf[...], sin_buf[...]

        def turned(r0):
            a = acc[r0:r0 + 64, :] * scale
            b = acc[r0 + 64:r0 + 128, :] * scale
            return a * cos - b * sin, b * cos + a * sin

        for hd in range(2):
            a, b = turned(hd * 128)
            q_out[hd * 128:hd * 128 + 64, :] = a.astype(BF16)
            q_out[hd * 128 + 64:hd * 128 + 128, :] = b.astype(BF16)

    def kv(slot, g):
        return kv_out.at[pl.ds(slot * 4 + g * 2, 2)]

    sib_slot = (4 * other, 4 - 2 * other, 2 - 2 * other)
    my_slot = (4 * c, 4 - 2 * c, 2 - 2 * c)

    def kv_way(n, g, src, dst, where):
        return remote(src, dst, k_ssem.at[n * 2 + g], k_rsem.at[n * 2 + g], where)

    def transit(g):
        return kv_via.at[pl.ds(g * 2, 2)]

    def kv_start():
        for g in range(2):
            src = kv_own.at[pl.ds(g * 2, 2)]

            @pl.when(y >= 2)
            def _():
                kv_way(5, g, src, transit(g), at_z(1)).start()

            @pl.when(y <= 2)
            def _():
                kv_way(0, g, src, kv(3, g), at_y(1)).start()

        for g in range(2):
            src = kv_own.at[pl.ds(g * 2, 2)]
            kv_way(2, g, src, kv(sib_slot[0], g), sibling).start()
        copy_here(kv_own, kv_out.at[pl.ds(20, 4)])

    def kv_transit(g):
        @pl.when(y == 3)
        def _():
            landed(transit(g), k_rsem.at[10 + g])
            kv_way(0, g, transit(g), kv(3, g), at_y(1)).start()

        @pl.when(y == 2)
        def _():
            landed(transit(g), k_rsem.at[10 + g])
            kv_way(6, g, transit(g), kv(1, g), at_y(2)).start()

    def kv_first(g):
        landed(kv(3, g), k_rsem.at[g])

        @pl.when(y <= 2)
        def _():
            kv_way(1, g, kv(3, g), kv(1, g), at_y(1)).start()

        kv_way(3, g, kv(3, g), kv(sib_slot[1], g), sibling).start()

    def kv_second(g):
        @pl.when(y >= 1)
        def _():
            landed(kv(1, g), k_rsem.at[2 + g])

        @pl.when(y == 0)
        def _():
            landed(kv(1, g), k_rsem.at[12 + g])

        kv_way(4, g, kv(1, g), kv(sib_slot[2], g), sibling).start()

    def kv_drain(g):
        own = kv_own.at[pl.ds(g * 2, 2)]
        kv_way(0, g, own, kv(3, g), sibling).wait_send()
        for n in (2, 3, 4):
            kv_way(n, g, own, kv(3, g), sibling).wait_send()

        @pl.when(y <= 2)
        def _():
            kv_way(1, g, own, kv(3, g), sibling).wait_send()

        @pl.when(y >= 2)
        def _():
            kv_way(5, g, own, kv(3, g), sibling).wait_send()

        @pl.when(y == 2)
        def _():
            kv_way(6, g, own, kv(3, g), sibling).wait_send()

    steps = {
        "W": turn_weights, "g1": gather.first, "g2": gather.second, "g3": gather.third, "sy": stage_y, "sc": stage_core,
        "sr": stage_reduce, "so": stage_root, "ss": stage_pass, "se": stage_end,
        "sz": stage_z, "sp": stage_spread, "sf": stage_far, "kt": kv_transit, "k1": kv_first, "k2": kv_second,
        "rot": lambda _: rotary_tables(), "kv": lambda _: kv_start(), "fin": lambda _: finish(), "q": lambda _: queries(),
        "M": lambda i: multiply(
            (l * 2 + x // 2, l * 2 + 1 - x // 2, (1 - l) * 2 + x // 2, (1 - l) * 2 + 1 - x // 2)[i], i == 0
        ),
    }
    groups = {"W": "mm", "M": "mm", "rot": "mm", "fin": "mm", "q": "mm", "g1": "gather", "g2": "gather", "g3": "gather",
              "kv": "kv", "kt": "kv", "k1": "kv", "k2": "kv"}
    for name, arg in SCHED:
        if groups.get(name, "prefix") in ON:
            steps[name](arg)
    if "prefix" in ON:
        for i in range(2):
            item = other + 2 * i
            for d in range(4):
                for h in range(2):
                    landed(quarter(item, (y + d) % 4, h), r_rsem.at[(i * 4 + d) * 2 + h])
    if "kv" in ON:
        for n in range(3):
            for g in range(2):
                landed(kv(my_slot[n], g), k_rsem.at[4 + 2 * n + g])
    gather.drain()
    for cp in pending:
        cp.wait_send()
    if "kv" in ON:
        for g in range(2):
            kv_drain(g)
    if "prefix" in ON:
        for h in range(2):
            end_drain(h)
    for cp in local[4 + (2 if "prefix" in ON else 0):]:
        cp.wait()


def kernel_attend(
    owner_s, len_s, order_s, pref_s, len_ref, order_ref, pref_ref, q_ref, kv_ref, f_ref, out_ref, acc, meta, work, item_of
):
    base = lax.axis_index("seq") * TOK
    seen = jnp.int32(0)
    for p in range(4):
        o = owner_s[p]
        inner = jnp.logical_and(o != 0, o != 31)
        item_of[p] = jnp.where(o == 0, 0, jnp.where(o == 31, 1, 2 + jnp.minimum(seen, 1)))
        seen = seen + inner.astype(jnp.int32)

    def look(r, carry):
        at = carry[0]
        req = order_s[r]
        stop = at + len_s[req]
        bit = jnp.int32(1) << pref_s[req]
        out = [stop]
        for rb in range(4):
            lo = base + rb * 128
            hit = jnp.logical_and(at < lo + 128, stop > lo)
            out.append(jnp.where(hit, carry[1 + 2 * rb] | bit, carry[1 + 2 * rb]))
            out.append(jnp.where(jnp.logical_and(at <= lo, stop > lo), at, carry[2 + 2 * rb]))
        return tuple(out)

    zero = jnp.int32(0)
    found = lax.fori_loop(0, REQS, look, (zero,) * 9)
    count = jnp.int32(0)
    for rb in range(4):
        for p in range(4):
            work[count] = rb * 4 + p
            count = count + ((found[1 + 2 * rb] >> p) & 1)

    first, stop, prefix = slot_tables(len_ref[...], order_ref[...], pref_ref[...])
    for rb in range(4):
        tok = (lax.broadcasted_iota(jnp.int32, (1, 256), 1) % 128 + (base + rb * 128)).astype(F32)
        begin = jnp.max(jnp.where(stop <= tok, jnp.broadcast_to(stop, (REQS, 256)), 0.0), axis=0, keepdims=True)
        inside = jnp.logical_and(first <= tok, tok < stop)
        pref = jnp.sum(jnp.where(inside, jnp.broadcast_to(prefix, (REQS, 256)), 0.0), axis=0, keepdims=True)
        meta[rb, 0:1, :] = tok
        meta[rb, 1:2, :] = begin
        meta[rb, 2:3, :] = pref
    c1 = float(QSCALE ** -0.5 / SOFTCAP)
    c2 = float(SOFTCAP * math.log2(math.e))
    ones = jnp.ones((16, KEYS), BF16)

    def queries(rb):
        lanes = pl.ds(pl.multiple_of(rb * 128, 128), 128)
        return jnp.concatenate([q_ref[0:128, lanes], q_ref[128:256, lanes]], axis=1)

    def weigh(k2, qt):
        sc = jnp.dot(k2, qt, preferred_element_type=F32)
        return jnp.exp2(jnp.tanh(sc * c1) * c2)

    for rb in range(4):
        qt = queries(rb)
        tok = meta[rb, 0:1, :]
        begin = meta[rb, 1:2, :]
        acc[rb] = jnp.zeros((144, 256), F32)
        chunks = (base + (rb + 1) * 128 - found[2 + 2 * rb] + KEYS - 1) // KEYS

        @pl.loop(0, chunks)
        def _(n):
            u = 20 + rb + 1 - (n + 1) * (KEYS // 128)
            k2 = jnp.concatenate([kv_ref[u + e, 0:128, :] for e in range(KEYS // 128)], axis=0)
            v2 = jnp.concatenate([kv_ref[u + e, 128:256, :] for e in range(KEYS // 128)], axis=1)
            key = (lax.broadcasted_iota(jnp.int32, (KEYS, 1), 0) + (base - 2560 + u * 128)).astype(F32)
            ok = jnp.logical_and(key <= tok, key >= begin)
            w = jnp.where(ok, weigh(k2, qt), 0.0).astype(BF16)
            acc[rb] += jnp.dot(jnp.concatenate([v2, ones], axis=0), w, preferred_element_type=F32)

    @pl.loop(0, count)
    def _(i):
        code = work[i]
        rb, p = code >> 2, code & 3
        item = item_of[p]
        qt = queries(rb)
        ws = []
        vs = []
        for n in range(PREFIX // KEYS):
            u = n * (KEYS // 64)
            k2 = jnp.concatenate([f_ref[item, u + 2 * e] for e in range(KEYS // 128)], axis=0)
            vs += [f_ref[item, u + 2 * e + 1] for e in range(KEYS // 128)]
            ws.append(weigh(k2, qt).astype(BF16))
        v2 = jnp.concatenate([jnp.concatenate(vs, axis=1), jnp.ones((16, PREFIX), BF16)], axis=0)
        part = jnp.dot(v2, jnp.concatenate(ws, axis=0), preferred_element_type=F32)
        acc[rb] += jnp.where(meta[rb, 2:3, :] == p.astype(F32), part, 0.0)

    for rb in range(4):
        lanes = slice(rb * 128, rb * 128 + 128)
        att = acc[rb, 0:128, :] / acc[rb, 128:129, :]
        out_ref[0:128, lanes] = att[:, 0:128].astype(BF16)
        out_ref[128:256, lanes] = att[:, 128:256].astype(BF16)


def kernel_out(
    att_ref, wo_hbm, h_ref, gain_ref, out_ref, g_buf, wo_buf, acc, gcol, sums, g_ssem, g_rsem, q_ssem, q_rsem, local_sem
):
    s = lax.axis_index("seq")
    t = lax.axis_index("tp")
    l, x = t // 4, t % 4
    gather = Gather(OUT_PIECES, att_ref, g_buf, g_ssem, g_rsem, 256, x, l)

    def peer(d):
        return {"tp": (t + d) % 8}

    barrier = pltpu.get_barrier_semaphore()
    for d in range(1, 8):
        pl.semaphore_signal(barrier, inc=1, device_id=peer(d), device_id_type=MESH)
    wo_copy = pltpu.make_async_copy(wo_hbm, wo_buf, local_sem.at[0])
    own_copy = pltpu.make_async_copy(att_ref, g_buf.at[pl.ds(pl.multiple_of(t * 256, 256), 256)], local_sem.at[1])
    wo_copy.start()
    own_copy.start()
    pl.semaphore_wait(barrier, 7)
    gather.start()

    g5 = gain_ref[t]
    for b in range(5):
        gcol[b * 128:(b + 1) * 128, :] = jnp.broadcast_to(g5[b:b + 1, :], (128, 128)).T
    wo_copy.wait()
    own_copy.wait()

    def multiply(dx, dl, begin):
        shard = ((l + dl) % 2) * 4 + (x + dx) % 4
        rows = pl.ds(pl.multiple_of(shard * 256, 256), 256)

        @pl.loop(0, 4)
        def _(m):
            mm = pl.ds(pl.multiple_of(m * 144, 16), 144)
            part = jnp.dot(wo_buf[mm, rows], g_buf[rows, :], preferred_element_type=F32)
            acc[mm, :] = part if begin else acc[mm, :] + part

    multiply(0, 0, True)
    for k in range(4):
        gather.first(k)
    multiply(1, 0, False)
    multiply(3, 0, False)
    multiply(0, 1, False)
    for k in range(4):
        gather.second(k)
    multiply(2, 0, False)
    multiply(1, 1, False)
    multiply(3, 1, False)
    for k in range(4):
        gather.third(k)
    multiply(2, 1, False)

    tot = jnp.zeros((8, TOK), F32)
    for b in range(72):
        v = acc[b * 8:(b + 1) * 8, :]
        tot = tot + v * v
    sums[t] = tot
    copies = []
    for d in range(1, 8):
        cp = remote(sums.at[t], sums.at[t], q_ssem.at[d - 1], q_rsem.at[7 - d], peer(d))
        cp.start()
        copies.append(cp)
    for d in range(1, 8):
        here = sums.at[(t + d) % 8]
        remote(here, here, q_ssem.at[0], q_rsem.at[d - 1], peer(1)).wait_recv()
    tot = sums[0]
    for d in range(1, 8):
        tot = tot + sums[d]
    scale = lax.rsqrt(jnp.sum(tot, axis=0, keepdims=True) * (1.0 / WIDTH) + EPS)
    for b in range(9):
        rows = slice(b * 64, b * 64 + 64)
        g = gcol[rows, :]
        for n in range(4):
            cols = slice(n * 128, n * 128 + 128)
            post = acc[rows, cols] * scale[:, cols] * g
            out_ref[rows, cols] = (h_ref[rows, cols].astype(F32) + post).astype(BF16)
    gather.drain()
    for cp in copies:
        cp.wait_send()


def on_device(
    hidden_in, pre_gain, post_gain, w_query, key_weight, value_weight, w_out, cache, suffix_len, request_order,
    request_prefix, prefix_owner,
):
    hbm = pl.BlockSpec(memory_space=pltpu.MemorySpace.HBM)
    vmem = pl.BlockSpec(memory_space=pltpu.VMEM)
    smem = pl.BlockSpec(memory_space=pltpu.SMEM)
    dma = pltpu.SemaphoreType.DMA
    h_t = hidden_in.T
    len_row = suffix_len.reshape(1, REQS)
    order_row = request_order.reshape(1, REQS)
    pref_row = request_prefix.reshape(1, REQS)
    freq = jnp.asarray((10000.0 ** (-2.0 * np.arange(64) / HEAD)).astype(np.float32).reshape(64, 1))
    n = len(IN_PIECES)
    sends = 7 * n
    one = pltpu.VMEM((128, 128), BF16)
    three = pltpu.VMEM((3, 128, 128), BF16)
    half = pltpu.VMEM((4, 128, 128), BF16)
    four = pltpu.VMEM((4, 4, 128, 128), BF16)
    two = pltpu.VMEM((2, 4, 128, 128), BF16)
    q, kv, spread = pl.pallas_call(
        kernel_in,
        out_shape=(
            jax.ShapeDtypeStruct((256, TOK), BF16),
            jax.ShapeDtypeStruct((24, 256, 128), BF16),
            jax.ShapeDtypeStruct((4, 32, 128, 128), BF16),
        ),
        in_specs=[smem, vmem, vmem, vmem, vmem, vmem, hbm, hbm, hbm, hbm, vmem],
        out_specs=(vmem, vmem, vmem),
        scratch_shapes=[
            pltpu.VMEM((WIDTH, TOK), BF16),
            pltpu.VMEM((WIDTH, 512), BF16),
            pltpu.VMEM((512, WIDTH), BF16),
            pltpu.VMEM((512, TOK), F32),
            pltpu.VMEM((8, TOK), F32),
            pltpu.VMEM((64, TOK), F32),
            pltpu.VMEM((64, TOK), F32),
            pltpu.VMEM((32, 128, 128), BF16),
            four, four, half, half, two, two, half, half, half, half, three, three, one, one,
            pltpu.VMEM((4, 256, 128), BF16), pltpu.VMEM((4, 256, 128), BF16),
            dma((sends,)), dma((8 * n,)), dma((6,)), dma((6,)), dma((2,)), dma((2,)), dma((12,)), dma((12,)),
            dma((12,)), dma((12,)), dma((4,)), dma((2,)), dma((2,)), dma((16,)), dma((16,)), dma((14,)), dma((14,)), dma((12,)),
        ],
        compiler_params=pltpu.CompilerParams(collective_id=0, has_side_effects=True, vmem_limit_bytes=34 << 20),
    )(
        prefix_owner, len_row, order_row, pref_row, pre_gain.reshape(36, 128), freq,
        h_t, w_query, key_weight, value_weight, cache.reshape(4096, 128),
    )
    att = pl.pallas_call(
        kernel_attend,
        out_shape=jax.ShapeDtypeStruct((256, TOK), BF16),
        in_specs=[smem] * 4 + [vmem] * 6,
        out_specs=vmem,
        scratch_shapes=[
            pltpu.VMEM((4, 144, 256), F32),
            pltpu.VMEM((4, 8, 256), F32),
            pltpu.SMEM((17,), jnp.int32),
            pltpu.SMEM((4,), jnp.int32),
        ],
        compiler_params=pltpu.CompilerParams(vmem_limit_bytes=16 << 20),
    )(prefix_owner, suffix_len, request_order, request_prefix, len_row, order_row, pref_row, q, kv, spread)
    gains = jnp.pad(post_gain.reshape(8, SHARD), ((0, 0), (0, 64))).reshape(8, 5, 128)
    out = pl.pallas_call(
        kernel_out,
        out_shape=jax.ShapeDtypeStruct((SHARD, TOK), BF16),
        in_specs=[vmem, hbm, vmem, vmem],
        out_specs=vmem,
        scratch_shapes=[
            pltpu.VMEM((2048, TOK), BF16),
            pltpu.VMEM((SHARD, 2048), BF16),
            pltpu.VMEM((SHARD, TOK), F32),
            pltpu.VMEM((640, 128), F32),
            pltpu.VMEM((8, 8, TOK), F32),
            dma((7 * len(OUT_PIECES),)), dma((8 * len(OUT_PIECES),)), dma((7,)), dma((7,)), dma((2,)),
        ],
        compiler_params=pltpu.CompilerParams(collective_id=1, has_side_effects=True, vmem_limit_bytes=16 << 20),
    )(att, w_out.T, h_t, gains)
    return out.T


def solution(mesh):
    placed = (
        P("seq", "tp"), P(), P(), P(None, "tp"), P(None, "tp"), P(None, "tp"), P(None, "tp"), P("seq", None, "tp"),
        P(), P(), P(), P(),
    )
    return jax.shard_map(on_device, mesh=mesh, in_specs=placed, out_specs=P("seq", "tp"), check_vma=False)
```

time: 173 us -> 130 us (0.75)
  the two profiles are of different devices: /device:TPU:73 before, /device:TPU:230 now
where the time goes in v2:
time: 130 us
  Pallas kernels  118 us (91%)
  local copies, waits for them, and re-layouts  11.5 us (9%)
    pallas_call x1, Pallas kernels, on_device(): pl.pallas_call(kernel_in, out_shape=(jax.ShapeDtypeStruct((256, TOK), BF1...  71.5 us
    pallas_call x1, Pallas kernels, on_device(): pl.pallas_call(kernel_out, out_shape=jax.ShapeDtypeStruct((SHARD, TOK), B...  34.1 us
    pallas_call x1, Pallas kernels, on_device(): pl.pallas_call(kernel_attend, out_shape=jax.ShapeDtypeStruct((256, TOK),...  12.8 us
    unnamed x29, local copies, waits for them, and re-layouts  11.4 us

profile of v2, /device:TPU:230, one launch (start us, length us, event | category | flops | bytes accessed | tf_op | source)
XLA Modules:
  0.0 130.0 jit_solution(5786236480960551250)
XLA Ops:
  0.0 0.0 copy-start
  0.0 1.7 %copy-done = bf16[4608,256]{1,0:T(8,128)(2,1)S(1)} copy-done((bf16[4608,256]{1,0:T(8,128)(2,1)S(1)}, bf16[4608,256]{1,0:T(8,128)(2,1)}, u32[]{:S(2)}) %copy-start) | copy-done | bytes 2359320
  1.7 0.0 copy-start.1
  1.7 1.1 copy-done.1
  2.7 1.3 copy-done.4
  4.0 1.3 copy-done.5
  5.3 1.2 copy-done.6
  6.5 0.8 copy-done.7
  7.3 0.7 copy-done.8
  8.0 0.7 copy-done.9
  8.6 0.7 copy-done.10
  9.3 0.7 copy-done.11
  10.0 0.7 copy-done.12
  10.6 71.5 %shard_map.127 = (bf16[256,512]{1,0:T(8,128)(2,1)S(1)}, bf16[24,256,128]{2,1,0:T(8,128)(2,1)S(1)}, bf16[4,32,128,128]{3,2,1,0:T(8,128)(2,1)S(1)}) custom-call(s32[4]{0:T(128)S(1)} %copy-done.12, s32[1,48]{1,0:T(1,128)S(1)} %bitcast.16, s32[1,48]{1,0:T(1,128)S(1)} %bitcast.18, s32[1,48]{1,0:T(1,128)S(1)} %bitcast.20, f32[36,128]{1,0:T(8,128)S(1)} %bitcast.15, ...), custom_call_target="tpu_custom_call" | custom-call | tf_op jit(solution)/shard_map/pallas_call | solution.py:746
  82.2 0.0 copy-start.13
  82.2 0.0 copy-start.2
  82.2 0.0 copy-start.3
  82.2 12.8 %shard_map.128.att_ref = bf16[256,512]{1,0:T(8,128)(2,1)S(1)} custom-call(s32[4]{0:T(128)S(1)} %copy-done.12, s32[48]{0:T(128)S(1)} %copy-done.9, s32[48]{0:T(128)S(1)} %copy-done.10, s32[48]{0:T(128)S(1)} %copy-done.11, s32[1,48]{1,0:T(1,128)S(1)} %bitcast.17, s32[1,48]{1,0:T(1,128)S(1)} %bitcast.19, s32[1,48]{1,0:T(1,128)S(1)} %bitcast.21, ...), custom_call_target="tpu_custom_call" | custom-call | tf_op jit(solution)/shard_map/pallas_call | solution.py:774
  95.0 0.0 copy-done.13
  95.0 0.1 reshape.26
  95.1 0.0 copy-done.2
  95.1 0.0 copy-done.3
  95.1 34.1 %shard_map.129 = bf16[576,512]{1,0:T(8,128)(2,1)S(1)} custom-call(bf16[256,512]{1,0:T(8,128)(2,1)S(1)} %shard_map.128.att_ref, bf16[576,2048]{1,0:T(8,128)(2,1)S(1)} %bitcast.12, bf16[576,512]{1,0:T(8,128)(2,1)S(1)} %bitcast.11, f32[8,5,128]{2,1,0:T(8,128)S(1)} %copy.14.gain_ref), custom_call_target="tpu_custom_call" | custom-call | tf_op jit(solution)/shard_map/pallas_call | solution.py:788
  129.2 0.8 copy.16
  (11 shorter events, 0.0 us)
Async XLA Ops:
  0.0 1.7 %copy-start = (bf16[4608,256]{1,0:T(8,128)(2,1)S(1)}, bf16[4608,256]{1,0:T(8,128)(2,1)}, u32[]{:S(2)}) copy-start(bf16[4608,256]{1,0:T(8,128)(2,1)} %wq_hbm.1) | copy-start | bytes 7077892
  1.7 1.1 copy-start.1
  2.7 1.3 copy-start.4
  4.0 1.3 copy-start.5
  5.3 1.2 copy-start.6
  6.5 0.8 copy-start.7
  7.3 0.7 copy-start.8
  8.0 0.7 copy-start.9
  8.6 0.7 copy-start.10
  9.3 0.7 copy-start.11
  10.0 0.7 copy-start.12
  82.2 12.8 %copy-start.13 = (f32[4608]{0:T(1024)S(1)}, f32[4608]{0:T(1024)}, u32[]{:S(2)}) copy-start(f32[4608]{0:T(1024)} %param.15) | copy-start | bytes 55300
  82.2 12.9 %copy-start.2 = (bf16[512,576]{0,1:T(8,128)(2,1)S(1)}, bf16[512,576]{0,1:T(8,128)(2,1)}, u32[]{:S(2)}) copy-start(bf16[512,576]{0,1:T(8,128)(2,1)} %param.13) | copy-start | bytes 1769476
  82.2 12.9 %copy-start.3 = (bf16[2048,576]{0,1:T(8,128)(2,1)S(1)}, bf16[2048,576]{0,1:T(8,128)(2,1)}, u32[]{:S(2)}) copy-start(bf16[2048,576]{0,1:T(8,128)(2,1)} %param.19) | copy-start | bytes 7077892

commit v3 on v2

--- a/solution.py
+++ b/solution.py
@@ -23,12 +23,14 @@
 KEYS = 512
 ON = ("mm", "gather", "prefix", "kv")
 SCHED = (
-    ("W", 0), ("g1", 0), ("sy", 0), ("sc", 0), ("W", 1), ("g1", 1), ("sr", 0), ("W", 2), ("g1", 2),
-    ("so", 0), ("sy", 1), ("sc", 1), ("W", 3), ("g1", 3), ("ss", 0), ("sr", 1), ("M", 0), ("rot", 0),
-    ("g2", 0), ("se", 0), ("sz", 0), ("so", 1), ("g2", 1), ("g2", 2), ("ss", 1), ("sp", 0), ("g2", 3),
-    ("M", 1), ("se", 1), ("sz", 1), ("M", 2), ("sf", 0), ("g3", 0), ("g3", 1), ("g3", 2), ("g3", 3),
-    ("M", 3), ("fin", 0), ("kv", 0), ("q", 0), ("sp", 1), ("kt", 0), ("kt", 1), ("k1", 0), ("k1", 1),
-    ("sf", 1), ("k2", 0), ("k2", 1),
+    ("W", 0), ("g1", 0), ("g1", 1), ("gs", 0), ("sy", 0), ("sc", 0), ("W", 1), ("sy", 1), ("g2", 0),
+    ("sc", 1), ("W", 2), ("er", 0), ("sy", 2), ("sr", 0), ("g2", 1), ("sc", 2), ("W", 3), ("er", 1),
+    ("sy", 3), ("sr", 1), ("g1", 2), ("sc", 3), ("M", 0), ("er", 2), ("se", 0), ("sz", 0), ("sr", 2),
+    ("g1", 3), ("rot", 0), ("er", 3), ("se", 1), ("sz", 1), ("sr", 3), ("M", 1), ("M", 2), ("g3", 0),
+    ("g3", 1), ("sp", 0), ("se", 2), ("sz", 2), ("M", 3), ("fin", 0), ("kv", 0), ("q", 0), ("se", 3),
+    ("sz", 3), ("sp", 1), ("sf", 0), ("g2", 2), ("M", 4), ("g2", 3), ("sp", 2), ("sf", 1), ("kt", 0),
+    ("M", 5), ("M", 6), ("sp", 3), ("sf", 2), ("k1", 0), ("sf", 3), ("g3", 2), ("k2", 0), ("g3", 3),
+    ("M", 7), ("fin", 1), ("kv", 1), ("q", 1), ("kt", 1), ("k1", 1), ("k2", 1),
 )
 F32 = jnp.float32
 BF16 = jnp.bfloat16
@@ -41,14 +43,15 @@
 
 
 class Gather:
-    def __init__(self, pieces, own, buf, ssem, rsem, rows, x, l):
+    def __init__(self, pieces, halves, own, buf, ssem, rsem, rows, x, l):
         self.pieces = pieces
         self.own, self.buf, self.ssem, self.rsem, self.rows = own, buf, ssem, rsem, rows
         self.x, self.l = x, l
         self.count = 0
         self.started = []
         self.n = len(pieces)
-        self.prow = rows // self.n
+        self.prow = rows // 2 if halves else rows // self.n
+        self.halves = halves
 
     def target(self, way):
         x, l = self.x, self.l
@@ -60,12 +63,18 @@
 
     def place(self, dx, dl, k):
         shard = ((self.l + dl) % 2) * 4 + (self.x + dx) % 4
-        return self.buf.at[pl.ds(pl.multiple_of(shard * self.rows + k * self.prow, 16), self.prow)]
+        return self.part(self.buf, shard * self.rows, k)
+
+    def part(self, ref, base, k):
+        if not self.halves:
+            return ref.at[pl.ds(pl.multiple_of(base + k * self.prow, 16), self.prow)]
+        rows = pl.ds(pl.multiple_of(base + (k % 2) * self.prow, 16), self.prow)
+        return ref.at[rows, pl.ds((k // 2) * (TOK // 2), TOK // 2)]
 
     def send(self, dx, dl, k, way):
         src = self.place(dx, dl, k)
         if dx == 0 and dl == 0:
-            src = self.own.at[pl.ds(k * self.prow, self.prow)]
+            src = self.part(self.own, 0, k)
         rdx, rdl = dx, dl
         if way == "R":
             rdx = (dx + 3) % 4
@@ -84,8 +93,8 @@
         here = self.place(dx, dl, k)
         remote(here, here, self.ssem.at[0], self.rsem.at[(dl * 4 + dx) * self.n + k], self.target("R")).wait_recv()
 
-    def start(self):
-        for k in range(self.n):
+    def start(self, k0, k1):
+        for k in range(k0, k1):
             for way in ("R", "L", "Z"):
                 self.send(0, 0, k, way)
 
@@ -139,15 +148,16 @@
     return stop - length, stop, prefix
 
 
-def kernel_in(
-    owner_ref, len_ref, order_ref, pref_ref, gain_ref, freq_ref,
-    h_hbm, wq_hbm, wk_hbm, wv_hbm, cache_ref,
-    q_out, kv_out, f_out,
-    h_buf, w_buf, wt, acc, sq, cos_buf, sin_buf, cache_f,
-    y0, y1, s0, s1, c0, c1, z0, z1, p0, p1, i0, i1, m0, m1, kv_own, kv_via,
-    g_ssem, g_rsem, y_ssem, y_rsem, b_ssem, b_rsem, z_ssem, z_rsem, t_ssem, t_rsem,
-    a_ssem, a_rsem, e_sem, r_ssem, r_rsem, k_ssem, k_rsem, local_sem,
-):
+def kernel_in(*refs):
+    (
+        owner_ref, len_ref, order_ref, pref_ref, gain_ref, freq_ref, h_hbm, wq_hbm, wk_hbm, wv_hbm, cache_hbm,
+        q_out, kv_out, f_out, h_buf, w_buf, wt, acc, sq, cos_buf, sin_buf, cache_buf, cache_f,
+    ) = refs[:23]
+    parts = refs[23:47]
+    (
+        kv_own, kv_via, g_ssem, g_rsem, y_ssem, y_rsem, b_ssem, b_rsem, z_ssem, z_rsem, t_ssem, t_rsem,
+        a_ssem, a_rsem, e_sem, r_ssem, r_rsem, k_ssem, k_rsem, local_sem,
+    ) = refs[47:]
     s = lax.axis_index("seq")
     t = lax.axis_index("tp")
     zh, y, c = s // 8, (s // 2) % 4, s % 2
@@ -161,11 +171,11 @@
     def at_z(d):
         return {"seq": ((zh + d) % 4) * 8 + y * 2 + c}
 
-    gather = Gather(IN_PIECES, h_hbm, h_buf, g_ssem, g_rsem, SHARD, x, l)
+    gather = Gather(IN_PIECES, True, h_hbm, h_buf, g_ssem, g_rsem, SHARD, x, l)
 
     barrier = pltpu.get_barrier_semaphore()
     peers = [gather.target("R"), gather.target("L"), gather.target("Z"), sibling]
-    peers += [at_y(1), at_y(2), at_y(3), at_z(1), at_z(3)]
+    peers += [at_y(1), at_y(2), at_y(3), at_z(1), at_z(2), at_z(3)]
     for peer in peers:
         pl.semaphore_signal(barrier, inc=1, device_id=peer, device_id_type=MESH)
 
@@ -177,6 +187,7 @@
         local.append(cp)
         return cp
 
+    cache_copy = copy_here(cache_hbm, cache_buf)
     weights = [
         copy_here(wq_hbm, w_buf.at[:, pl.ds(0, 256)]),
         copy_here(wk_hbm, w_buf.at[:, pl.ds(256, 128)]),
@@ -185,25 +196,25 @@
     ]
     pl.semaphore_wait(barrier, len(peers))
     if "gather" in ON:
-        gather.start()
+        gather.start(0, 2)
 
     to = lax.broadcasted_iota(jnp.int32, (256, 256), 0)
     of = lax.broadcasted_iota(jnp.int32, (256, 256), 1)
     apart = jnp.where(of == 2 * to - jnp.where(to < 128, 0, 255), 1.0, 0.0).astype(BF16)
 
-    def split_cache(b0, b1):
-        @pl.loop(b0, b1)
-        def _(b):
-            rows = pl.ds(pl.multiple_of(b * 256, 256), 256)
-            both = jnp.dot(apart, cache_ref[rows, :], preferred_element_type=F32)
-            cache_f[b * 2] = both[0:128].astype(BF16)
-            cache_f[b * 2 + 1] = both[128:256].T.astype(BF16)
-
-    if "prefix" in ON:
-        split_cache(0, 16)
-
-    halves = ((y0, s0, c0, z0, p0), (y1, s1, c1, z1, p1))
-    zin, zmid = (i0, i1), (m0, m1)
+    def split_cache(h):
+        for j in range(4):
+            b = j * 4 + h
+            both = jnp.dot(apart, cache_buf[b * 256:(b + 1) * 256, :], preferred_element_type=F32)
+            values = both[128:256].T.astype(BF16)
+            for e in range(2):
+                cache_f[b * 4 + e] = both[e * 64:e * 64 + 64].astype(BF16)
+                cache_f[b * 4 + 2 + e] = values[e * 64:e * 64 + 64]
+
+    cache_copy.wait()
+
+    halves = [parts[h * 6:h * 6 + 5] for h in range(4)]
+    zin = [parts[h * 6 + 5] for h in range(4)]
     pending = []
 
     def push(src, dst, ssem, rsem, where):
@@ -215,12 +226,13 @@
         remote(ref, ref, y_ssem.at[0], rsem, sibling).wait_recv()
 
     own_y = []
-    for h in (range(2) if "prefix" in ON else ()):
+    for h in (range(4) if "prefix" in ON else ()):
         yb = halves[h][0]
+        split_cache(h)
         for d in (1, 3, 2):
             j = (y + d) % 4
-            push(cache_f.at[pl.ds(j * 8 + h * 4, 4)], yb.at[y], y_ssem.at[h * 3 + d - 1], y_rsem.at[h * 3 + 3 - d], at_y(d))
-        own_y.append(copy_here(cache_f.at[pl.ds(y * 8 + h * 4, 4)], yb.at[y]))
+            push(cache_f.at[pl.ds(j * 16 + h * 4, 4)], yb.at[y], y_ssem.at[h * 3 + d - 1], y_rsem.at[h * 3 + 3 - d], at_y(d))
+        own_y.append(copy_here(cache_f.at[pl.ds(y * 16 + h * 4, 4)], yb.at[y]))
 
     oc = jnp.int32(-1)
     od = jnp.int32(-1)
@@ -236,7 +248,7 @@
     theirs = jnp.where(c == 0, od, oc)
 
     def quarter(item, j, h):
-        return f_out.at[item, pl.ds(j * 8 + h * 4, 4)]
+        return f_out.at[item, pl.ds(j * 16 + h * 4, 4)]
 
     far = (zh - 3 * c) % 4
 
@@ -269,48 +281,39 @@
         yb, sb, cb, zb, pb = halves[h]
         landed(cb.at[other], b_rsem.at[h])
         zb[...] = cb[mine & 1]
-        push(unit(zb, 2), zin[h].at[0], zsem(z_ssem, h, 0), zsem(z_rsem, h, 0), at_z(3))
-        push(unit(zb, 3), zin[h].at[1], zsem(z_ssem, h, 1), zsem(z_rsem, h, 1), at_z(1))
+        for d in (1, 3, 2):
+            push(unit(zb, d), zin[h].at[d - 1], zsem(z_ssem, h, d - 1), zsem(z_rsem, h, d - 1), at_z(4 - d))
 
     zo = mine >> 3
 
     def stage_reduce(h):
         yb, sb, cb, zb, pb = halves[h]
-        landed(zin[h].at[0], zsem(z_rsem, h, 0))
-        zmid[h][...] = jnp.where(zo == (zh + 1) % 4, zin[h][0], zb[(zh + 3) % 4])
-        push(zmid[h], zin[h].at[2], zsem(z_ssem, h, 2), zsem(z_rsem, h, 2), at_z(3))
-
+        whole = zb[zh]
+        for d in (1, 3, 2):
+            landed(zin[h].at[d - 1], zsem(z_rsem, h, d - 1))
+            whole = jnp.where(zo == (zh + d) % 4, zin[h][d - 1], whole)
+        pb[zh] = whole
+        for d in (1, 3, 2):
+            push(unit(pb, 0), unit(pb, 0), zsem(z_ssem, h, 2 + d), zsem(z_rsem, h, 2 + d), at_z(d))
+
+    def stage_relay(h):
         @pl.when(jnp.logical_or(far == 1, far == 3))
         def _():
             landed(quarter(c, y, h), a_rsem.at[h])
 
-        @pl.when(far == (1 if h == 0 else 3))
-        def _():
-            end_copy(h, 1 if h == 0 else 3, quarter(c, y, h)).start()
-
-    def stage_root(h):
-        yb, sb, cb, zb, pb = halves[h]
-        landed(zin[h].at[1], zsem(z_rsem, h, 1))
-        landed(zin[h].at[2], zsem(z_rsem, h, 2))
-        whole = jnp.where(zo == zh, zb[zh], jnp.where(zo == (zh + 3) % 4, zin[h][1], zin[h][2]))
-        pb[zh] = whole
-        push(unit(pb, 0), unit(pb, 0), zsem(z_ssem, h, 3), zsem(z_rsem, h, 3), at_z(1))
-        push(unit(pb, 0), unit(pb, 0), zsem(z_ssem, h, 4), zsem(z_rsem, h, 4), at_z(3))
+        @pl.when(far == (1 if h % 2 == 0 else 3))
+        def _():
+            end_copy(h, 1 if h % 2 == 0 else 3, quarter(c, y, h)).start()
 
     def relay(item, j, h, i, d):
-        n = (i * 4 + d) * 2 + h
+        n = (i * 4 + d) * 4 + h
         push(quarter(item, j, h), quarter(item, j, h), r_ssem.at[n], r_rsem.at[n], sibling)
-
-    def stage_pass(h):
-        yb, sb, cb, zb, pb = halves[h]
-        landed(unit(pb, 1), zsem(z_rsem, h, 3))
-        push(unit(pb, 1), unit(pb, 1), zsem(z_ssem, h, 5), zsem(z_rsem, h, 5), at_z(1))
 
     def spread_own(h, i, src):
         item = c + 2 * i
         for d in (1, 3):
-            push(src, quarter(item, y, h), t_ssem.at[(i * 3 + d - 1) * 2 + h], t_rsem.at[(i * 3 + 3 - d) * 2 + h], at_y(d))
-        n = (i * 4) * 2 + h
+            push(src, quarter(item, y, h), t_ssem.at[(i * 3 + d - 1) * 4 + h], t_rsem.at[(i * 3 + 3 - d) * 4 + h], at_y(d))
+        n = (i * 4) * 4 + h
         push(src, quarter(item, y, h), r_ssem.at[n], r_rsem.at[n], sibling)
 
     def stage_end(h):
@@ -328,8 +331,8 @@
 
     def stage_z(h):
         yb, sb, cb, zb, pb = halves[h]
-        landed(unit(pb, 3), zsem(z_rsem, h, 4))
-        landed(unit(pb, 2), zsem(z_rsem, h, 5))
+        for d in (1, 3, 2):
+            landed(unit(pb, d), zsem(z_rsem, h, 2 + d))
         copy_here(pb, quarter(c + 2, y, h))
         spread_own(h, 1, pb)
 
@@ -339,19 +342,19 @@
             end_copy(h, 1, quarter(c, y, h)).wait_send()
             end_copy(h, 3, quarter(c, y, h)).wait_send()
 
-        @pl.when(far == (1 if h == 0 else 3))
-        def _():
-            end_copy(h, 1 if h == 0 else 3, quarter(c, y, h)).wait_send()
+        @pl.when(far == (1 if h % 2 == 0 else 3))
+        def _():
+            end_copy(h, 1 if h % 2 == 0 else 3, quarter(c, y, h)).wait_send()
 
     def stage_spread(h):
         for i in range(2):
             item = c + 2 * i
             for d in (3, 1):
                 j = (y + d) % 4
-                landed(quarter(item, j, h), t_rsem.at[(i * 3 + d - 1) * 2 + h])
+                landed(quarter(item, j, h), t_rsem.at[(i * 3 + d - 1) * 4 + h])
                 if (i == 0 and d == 3) or (i == 1 and d == 1):
                     push(
-                        quarter(item, j, h), quarter(item, j, h), t_ssem.at[(i * 3 + 1) * 2 + h], t_rsem.at[(i * 3 + 1) * 2 + h],
+                        quarter(item, j, h), quarter(item, j, h), t_ssem.at[(i * 3 + 1) * 4 + h], t_rsem.at[(i * 3 + 1) * 4 + h],
                         at_y(1 if i == 0 else 3),
                     )
                 relay(item, j, h, i, d)
@@ -360,7 +363,7 @@
         for i in range(2):
             item = c + 2 * i
             j = (y + 2) % 4
-            landed(quarter(item, j, h), t_rsem.at[(i * 3 + 1) * 2 + h])
+            landed(quarter(item, j, h), t_rsem.at[(i * 3 + 1) * 4 + h])
             relay(item, j, h, i, 2)
 
     def rotary_tables():
@@ -381,57 +384,49 @@
                 w = w_buf[rows, cb * 128:(cb + 1) * 128].astype(F32).T
                 wt[cb * 128:(cb + 1) * 128, rows] = (w * g).astype(BF16)
 
-    def multiply(pair, begin):
+    def multiply(pair, g, begin):
         rows = pl.multiple_of(pair * 1152, 128)
-
-        @pl.loop(0, 2)
-        def _(m):
-            mm = pl.ds(pl.multiple_of(m * 256, 256), 256)
-            part = jnp.dot(wt[mm, pl.ds(rows, 1152)], h_buf[pl.ds(rows, 1152), :], preferred_element_type=F32)
-            acc[mm, :] = part if begin else acc[mm, :] + part
+        lanes = slice(g * 256, g * 256 + 256)
+        for m in range(2):
+            mm = slice(m * 256, m * 256 + 256)
+            part = jnp.dot(wt[mm, pl.ds(rows, 1152)], h_buf[pl.ds(rows, 1152), lanes], preferred_element_type=F32)
+            acc[mm, lanes] = part if begin else acc[mm, lanes] + part
 
         @pl.loop(0, 9)
         def _(b):
-            v = h_buf[pl.ds(pl.multiple_of(rows + b * 128, 128), 128), :].astype(F32)
+            v = h_buf[pl.ds(pl.multiple_of(rows + b * 128, 128), 128), lanes].astype(F32)
             v = v * v
             tot = v[0:8]
             for e in range(1, 16):
                 tot = tot + v[e * 8:(e + 1) * 8]
-            sq[...] = sq[...] + tot
+            sq[:, lanes] = sq[:, lanes] + tot
 
     sq[...] = jnp.zeros_like(sq)
     for cp in weights:
         cp.wait()
 
-    def finish():
-        scale = lax.rsqrt(jnp.sum(sq[...], axis=0, keepdims=True) * (1.0 / WIDTH) + EPS)
-        cos, sin = cos_buf[...], sin_buf[...]
-
-        def turned(r0):
-            a = acc[r0:r0 + 64, :] * scale
-            b = acc[r0 + 64:r0 + 128, :] * scale
-            return a * cos - b * sin, b * cos + a * sin
-
-        a, b = turned(256)
+    def turned(r0, g):
+        lanes = slice(g * 256, g * 256 + 256)
+        scale = lax.rsqrt(jnp.sum(sq[:, lanes], axis=0, keepdims=True) * (1.0 / WIDTH) + EPS)
+        cos, sin = cos_buf[:, lanes], sin_buf[:, lanes]
+        a = acc[r0:r0 + 64, lanes] * scale
+        b = acc[r0 + 64:r0 + 128, lanes] * scale
+        return a * cos - b * sin, b * cos + a * sin, scale
+
+    def finish(g):
+        a, b, scale = turned(256, g)
         kt = jnp.concatenate([a, b], axis=0)
-        vt = (acc[384:512, :] * scale).astype(BF16)
-        for blk in range(4):
-            kv_own[blk, 0:128, :] = kt[:, blk * 128:(blk + 1) * 128].T.astype(BF16)
-            kv_own[blk, 128:256, :] = vt[:, blk * 128:(blk + 1) * 128]
-
-    def queries():
-        scale = lax.rsqrt(jnp.sum(sq[...], axis=0, keepdims=True) * (1.0 / WIDTH) + EPS)
-        cos, sin = cos_buf[...], sin_buf[...]
-
-        def turned(r0):
-            a = acc[r0:r0 + 64, :] * scale
-            b = acc[r0 + 64:r0 + 128, :] * scale
-            return a * cos - b * sin, b * cos + a * sin
-
+        vt = (acc[384:512, g * 256:g * 256 + 256] * scale).astype(BF16)
+        for e in range(2):
+            kv_own[g * 2 + e, 0:128, :] = kt[:, e * 128:(e + 1) * 128].T.astype(BF16)
+            kv_own[g * 2 + e, 128:256, :] = vt[:, e * 128:(e + 1) * 128]
+
+    def queries(g):
+        lanes = slice(g * 256, g * 256 + 256)
         for hd in range(2):
-            a, b = turned(hd * 128)
-            q_out[hd * 128:hd * 128 + 64, :] = a.astype(BF16)
-            q_out[hd * 128 + 64:hd * 128 + 128, :] = b.astype(BF16)
+            a, b, _ = turned(hd * 128, g)
+            q_out[hd * 128:hd * 128 + 64, lanes] = a.astype(BF16)
+            q_out[hd * 128 + 64:hd * 128 + 128, lanes] = b.astype(BF16)
 
     def kv(slot, g):
         return kv_out.at[pl.ds(slot * 4 + g * 2, 2)]
@@ -445,49 +440,47 @@
     def transit(g):
         return kv_via.at[pl.ds(g * 2, 2)]
 
-    def kv_start():
-        for g in range(2):
-            src = kv_own.at[pl.ds(g * 2, 2)]
-
-            @pl.when(y >= 2)
-            def _():
-                kv_way(5, g, src, transit(g), at_z(1)).start()
-
-            @pl.when(y <= 2)
-            def _():
-                kv_way(0, g, src, kv(3, g), at_y(1)).start()
-
-        for g in range(2):
-            src = kv_own.at[pl.ds(g * 2, 2)]
-            kv_way(2, g, src, kv(sib_slot[0], g), sibling).start()
-        copy_here(kv_own, kv_out.at[pl.ds(20, 4)])
+    def kv_start(g):
+        src = kv_own.at[pl.ds(g * 2, 2)]
+
+        @pl.when(y >= 2)
+        def _():
+            kv_way(5, g, src, transit(g), at_z(1)).start()
+
+        @pl.when(y <= 2)
+        def _():
+            kv_way(0, g, src, kv(3, g), at_y(1)).start()
+
+        kv_way(2, g, src, kv(sib_slot[0], g), sibling).start()
+        copy_here(src, kv_out.at[pl.ds(20 + g * 2, 2)])
 
     def kv_transit(g):
-        @pl.when(y == 3)
-        def _():
-            landed(transit(g), k_rsem.at[10 + g])
-            kv_way(0, g, transit(g), kv(3, g), at_y(1)).start()
-
-        @pl.when(y == 2)
+        @pl.when(y >= 2)
         def _():
             landed(transit(g), k_rsem.at[10 + g])
             kv_way(6, g, transit(g), kv(1, g), at_y(2)).start()
 
+        @pl.when(y == 3)
+        def _():
+            kv_way(0, g, transit(g), kv(3, g), at_y(1)).start()
+
+    passes = jnp.logical_or(y == 1, y == 2)
+
     def kv_first(g):
         landed(kv(3, g), k_rsem.at[g])
 
-        @pl.when(y <= 2)
+        @pl.when(passes)
         def _():
             kv_way(1, g, kv(3, g), kv(1, g), at_y(1)).start()
 
         kv_way(3, g, kv(3, g), kv(sib_slot[1], g), sibling).start()
 
     def kv_second(g):
-        @pl.when(y >= 1)
+        @pl.when(y >= 2)
         def _():
             landed(kv(1, g), k_rsem.at[2 + g])
 
-        @pl.when(y == 0)
+        @pl.when(y <= 1)
         def _():
             landed(kv(1, g), k_rsem.at[12 + g])
 
@@ -499,28 +492,25 @@
         for n in (2, 3, 4):
             kv_way(n, g, own, kv(3, g), sibling).wait_send()
 
-        @pl.when(y <= 2)
+        @pl.when(passes)
         def _():
             kv_way(1, g, own, kv(3, g), sibling).wait_send()
 
         @pl.when(y >= 2)
         def _():
             kv_way(5, g, own, kv(3, g), sibling).wait_send()
-
-        @pl.when(y == 2)
-        def _():
             kv_way(6, g, own, kv(3, g), sibling).wait_send()
 
     steps = {
         "W": turn_weights, "g1": gather.first, "g2": gather.second, "g3": gather.third, "sy": stage_y, "sc": stage_core,
-        "sr": stage_reduce, "so": stage_root, "ss": stage_pass, "se": stage_end,
+        "sr": stage_reduce, "er": stage_relay, "se": stage_end,
         "sz": stage_z, "sp": stage_spread, "sf": stage_far, "kt": kv_transit, "k1": kv_first, "k2": kv_second,
-        "rot": lambda _: rotary_tables(), "kv": lambda _: kv_start(), "fin": lambda _: finish(), "q": lambda _: queries(),
+        "rot": lambda _: rotary_tables(), "kv": kv_start, "fin": finish, "q": queries, "gs": lambda _: gather.start(2, 4),
         "M": lambda i: multiply(
-            (l * 2 + x // 2, l * 2 + 1 - x // 2, (1 - l) * 2 + x // 2, (1 - l) * 2 + 1 - x // 2)[i], i == 0
+            (l * 2 + x // 2, l * 2 + 1 - x // 2, (1 - l) * 2 + x // 2, (1 - l) * 2 + 1 - x // 2)[i % 4], i // 4, i % 4 == 0
         ),
     }
-    groups = {"W": "mm", "M": "mm", "rot": "mm", "fin": "mm", "q": "mm", "g1": "gather", "g2": "gather", "g3": "gather",
+    groups = {"W": "mm", "M": "mm", "rot": "mm", "fin": "mm", "q": "mm", "g1": "gather", "gs": "gather", "g2": "gather", "g3": "gather",
               "kv": "kv", "kt": "kv", "k1": "kv", "k2": "kv"}
     for name, arg in SCHED:
         if groups.get(name, "prefix") in ON:
@@ -529,8 +519,8 @@
         for i in range(2):
             item = other + 2 * i
             for d in range(4):
-                for h in range(2):
-                    landed(quarter(item, (y + d) % 4, h), r_rsem.at[(i * 4 + d) * 2 + h])
+                for h in range(4):
+                    landed(quarter(item, (y + d) % 4, h), r_rsem.at[(i * 4 + d) * 4 + h])
     if "kv" in ON:
         for n in range(3):
             for g in range(2):
@@ -542,9 +532,9 @@
         for g in range(2):
             kv_drain(g)
     if "prefix" in ON:
-        for h in range(2):
+        for h in range(4):
             end_drain(h)
-    for cp in local[4 + (2 if "prefix" in ON else 0):]:
+    for cp in local[5 + (4 if "prefix" in ON else 0):]:
         cp.wait()
 
 
@@ -627,9 +617,11 @@
         ws = []
         vs = []
         for n in range(PREFIX // KEYS):
-            u = n * (KEYS // 64)
-            k2 = jnp.concatenate([f_ref[item, u + 2 * e] for e in range(KEYS // 128)], axis=0)
-            vs += [f_ref[item, u + 2 * e + 1] for e in range(KEYS // 128)]
+            u = n * (KEYS // 32)
+            k2 = jnp.concatenate([f_ref[item, u + 4 * (e // 2) + e % 2] for e in range(KEYS // 64)], axis=0)
+            vs += [
+                jnp.concatenate([f_ref[item, u + 4 * e + 2], f_ref[item, u + 4 * e + 3]], axis=0) for e in range(KEYS // 128)
+            ]
             ws.append(weigh(k2, qt).astype(BF16))
         v2 = jnp.concatenate([jnp.concatenate(vs, axis=1), jnp.ones((16, PREFIX), BF16)], axis=0)
         part = jnp.dot(v2, jnp.concatenate(ws, axis=0), preferred_element_type=F32)
@@ -648,7 +640,7 @@
     s = lax.axis_index("seq")
     t = lax.axis_index("tp")
     l, x = t // 4, t % 4
-    gather = Gather(OUT_PIECES, att_ref, g_buf, g_ssem, g_rsem, 256, x, l)
+    gather = Gather(OUT_PIECES, False, att_ref, g_buf, g_ssem, g_rsem, 256, x, l)
 
     def peer(d):
         return {"tp": (t + d) % 8}
@@ -661,7 +653,7 @@
     wo_copy.start()
     own_copy.start()
     pl.semaphore_wait(barrier, 7)
-    gather.start()
+    gather.start(0, 4)
 
     g5 = gain_ref[t]
     for b in range(5):
@@ -698,7 +690,7 @@
     for b in range(72):
         v = acc[b * 8:(b + 1) * 8, :]
         tot = tot + v * v
-    sums[t] = tot
+    sums[t] = jnp.sum(tot, axis=0, keepdims=True)
     copies = []
     for d in range(1, 8):
         cp = remote(sums.at[t], sums.at[t], q_ssem.at[d - 1], q_rsem.at[7 - d], peer(d))
@@ -710,7 +702,7 @@
     tot = sums[0]
     for d in range(1, 8):
         tot = tot + sums[d]
-    scale = lax.rsqrt(jnp.sum(tot, axis=0, keepdims=True) * (1.0 / WIDTH) + EPS)
+    scale = lax.rsqrt(tot * (1.0 / WIDTH) + EPS)
     for b in range(9):
         rows = slice(b * 64, b * 64 + 64)
         g = gcol[rows, :]
@@ -738,19 +730,18 @@
     freq = jnp.asarray((10000.0 ** (-2.0 * np.arange(64) / HEAD)).astype(np.float32).reshape(64, 1))
     n = len(IN_PIECES)
     sends = 7 * n
-    one = pltpu.VMEM((128, 128), BF16)
-    three = pltpu.VMEM((3, 128, 128), BF16)
-    half = pltpu.VMEM((4, 128, 128), BF16)
-    four = pltpu.VMEM((4, 4, 128, 128), BF16)
-    two = pltpu.VMEM((2, 4, 128, 128), BF16)
+    part = [
+        pltpu.VMEM((4, 4, 64, 128), BF16), pltpu.VMEM((4, 64, 128), BF16), pltpu.VMEM((2, 4, 64, 128), BF16),
+        pltpu.VMEM((4, 64, 128), BF16), pltpu.VMEM((4, 64, 128), BF16), pltpu.VMEM((3, 64, 128), BF16),
+    ]
     q, kv, spread = pl.pallas_call(
         kernel_in,
         out_shape=(
             jax.ShapeDtypeStruct((256, TOK), BF16),
             jax.ShapeDtypeStruct((24, 256, 128), BF16),
-            jax.ShapeDtypeStruct((4, 32, 128, 128), BF16),
+            jax.ShapeDtypeStruct((4, 64, 64, 128), BF16),
         ),
-        in_specs=[smem, vmem, vmem, vmem, vmem, vmem, hbm, hbm, hbm, hbm, vmem],
+        in_specs=[smem, vmem, vmem, vmem, vmem, vmem, hbm, hbm, hbm, hbm, hbm],
         out_specs=(vmem, vmem, vmem),
         scratch_shapes=[
             pltpu.VMEM((WIDTH, TOK), BF16),
@@ -760,16 +751,22 @@
             pltpu.VMEM((8, TOK), F32),
             pltpu.VMEM((64, TOK), F32),
             pltpu.VMEM((64, TOK), F32),
-            pltpu.VMEM((32, 128, 128), BF16),
-            four, four, half, half, two, two, half, half, half, half, three, three, one, one,
+            pltpu.VMEM((4096, 128), BF16),
+            pltpu.VMEM((64, 64, 128), BF16),
+            *(part * 4),
             pltpu.VMEM((4, 256, 128), BF16), pltpu.VMEM((4, 256, 128), BF16),
-            dma((sends,)), dma((8 * n,)), dma((6,)), dma((6,)), dma((2,)), dma((2,)), dma((12,)), dma((12,)),
-            dma((12,)), dma((12,)), dma((4,)), dma((2,)), dma((2,)), dma((16,)), dma((16,)), dma((14,)), dma((14,)), dma((12,)),
+            dma((sends,)), dma((8 * n,)), dma((12,)), dma((12,)), dma((4,)), dma((4,)), dma((24,)), dma((24,)),
+            dma((24,)), dma((24,)), dma((8,)), dma((4,)), dma((4,)), dma((32,)), dma((32,)), dma((14,)), dma((14,)), dma((16,)),
         ],
         compiler_params=pltpu.CompilerParams(collective_id=0, has_side_effects=True, vmem_limit_bytes=34 << 20),
     )(
-        prefix_owner, len_row, order_row, pref_row, pre_gain.reshape(36, 128), freq,
-        h_t, w_query, key_weight, value_weight, cache.reshape(4096, 128),
+        *(
+            pltpu.with_memory_space_constraint(a, pltpu.MemorySpace.HBM)
+            for a in (
+                prefix_owner, len_row, order_row, pref_row, pre_gain.reshape(36, 128), freq,
+                h_t, w_query, key_weight, value_weight, cache.reshape(4096, 128),
+            )
+        )
     )
     att = pl.pallas_call(
         kernel_attend,
@@ -795,7 +792,7 @@
             pltpu.VMEM((SHARD, 2048), BF16),
             pltpu.VMEM((SHARD, TOK), F32),
             pltpu.VMEM((640, 128), F32),
-            pltpu.VMEM((8, 8, TOK), F32),
+            pltpu.VMEM((8, 1, TOK), F32),
             dma((7 * len(OUT_PIECES),)), dma((8 * len(OUT_PIECES),)), dma((7,)), dma((7,)), dma((2,)),
         ],
         compiler_params=pltpu.CompilerParams(collective_id=1, has_side_effects=True, vmem_limit_bytes=16 << 20),

time: 130 us -> 117 us (0.900)
  the two profiles are of different devices: /device:TPU:230 before, /device:TPU:2 now
where the time goes in v3:
time: 117 us
  Pallas kernels  116 us (99%)
    pallas_call x1, Pallas kernels, on_device(): pl.pallas_call(kernel_in, out_shape=(jax.ShapeDtypeStruct((256, TOK), BF1...  81.9 us
    pallas_call x1, Pallas kernels, on_device(): pl.pallas_call(kernel_out, out_shape=jax.ShapeDtypeStruct((SHARD, TOK), B...  25.2 us
    pallas_call x1, Pallas kernels, on_device(): pl.pallas_call(kernel_attend, out_shape=jax.ShapeDtypeStruct((256, TOK),...  9.05 us

profile of v3, /device:TPU:2, one launch (start us, length us, event | category | flops | bytes accessed | tf_op | source)
XLA Modules:
  0.0 117.2 jit_solution(9137382118415233970)
XLA Ops:
  0.0 0.0 copy-start.2
  0.0 0.0 copy-start.3
  0.0 0.0 copy-start.4
  0.0 0.0 copy-start.5
  0.0 81.9 %shard_map.127 = (bf16[256,512]{1,0:T(8,128)(2,1)S(1)}, bf16[24,256,128]{2,1,0:T(8,128)(2,1)S(1)}, bf16[4,64,64,128]{3,2,1,0:T(8,128)(2,1)S(1)}) custom-call(s32[4]{0:T(128)} %owner_s.1, s32[1,48]{1,0:T(1,128)} %bitcast.14, s32[1,48]{1,0:T(1,128)} %bitcast.16, s32[1,48]{1,0:T(1,128)} %bitcast.18, f32[36,128]{1,0:T(8,128)} %bitcast.21, ...), custom_call_target="tpu_custom_call" | custom-call | tf_op jit(solution)/shard_map/pallas_call | solution.py:737
  81.9 0.0 copy-done.2
  81.9 0.0 copy-done.3
  81.9 0.0 copy-done.4
  82.0 0.0 copy-done.5
  82.0 0.0 copy-start.6
  82.0 0.0 copy-start
  82.0 0.0 copy-start.1
  82.0 9.1 %shard_map.128.att_ref = bf16[256,512]{1,0:T(8,128)(2,1)S(1)} custom-call(s32[4]{0:T(128)S(1)} %copy-done.5, s32[48]{0:T(128)S(1)} %copy-done.2, s32[48]{0:T(128)S(1)} %copy-done.3, s32[48]{0:T(128)S(1)} %copy-done.4, s32[1,48]{1,0:T(1,128)S(1)} %bitcast.15, s32[1,48]{1,0:T(1,128)S(1)} %bitcast.17, s32[1,48]{1,0:T(1,128)S(1)} %bitcast.19, ...), custom_call_target="tpu_custom_call" | custom-call | tf_op jit(solution)/shard_map/pallas_call | solution.py:771
  91.1 0.0 copy-done.6
  91.1 0.1 reshape.26
  91.2 0.0 copy-done
  91.2 0.0 copy-done.1
  91.2 25.2 %shard_map.129 = bf16[576,512]{1,0:T(8,128)(2,1)S(1)} custom-call(bf16[256,512]{1,0:T(8,128)(2,1)S(1)} %shard_map.128.att_ref, bf16[576,2048]{1,0:T(8,128)(2,1)S(1)} %bitcast.12, bf16[576,512]{1,0:T(8,128)(2,1)S(1)} %bitcast.11, f32[8,5,128]{2,1,0:T(8,128)S(1)} %copy.14.gain_ref), custom_call_target="tpu_custom_call" | custom-call | tf_op jit(solution)/shard_map/pallas_call | solution.py:785
  116.4 0.8 copy.16
  (2 shorter events, 0.0 us)
Async XLA Ops:
  0.0 81.9 %copy-start.2 = (s32[48]{0:T(128)S(1)}, s32[48]{0:T(128)}, u32[]{:S(2)}) copy-start(s32[48]{0:T(128)} %len_s.1) | copy-start | bytes 580
  0.0 81.9 %copy-start.3 = (s32[48]{0:T(128)S(1)}, s32[48]{0:T(128)}, u32[]{:S(2)}) copy-start(s32[48]{0:T(128)} %order_s.1) | copy-start | bytes 580
  0.0 81.9 %copy-start.4 = (s32[48]{0:T(128)S(1)}, s32[48]{0:T(128)}, u32[]{:S(2)}) copy-start(s32[48]{0:T(128)} %pref_s.1) | copy-start | bytes 580
  0.0 81.9 %copy-start.5 = (s32[4]{0:T(128)S(1)}, s32[4]{0:T(128)}, u32[]{:S(2)}) copy-start(s32[4]{0:T(128)} %owner_s.1) | copy-start | bytes 52
  82.0 9.1 %copy-start.6 = (f32[4608]{0:T(1024)S(1)}, f32[4608]{0:T(1024)}, u32[]{:S(2)}) copy-start(f32[4608]{0:T(1024)} %param.15) | copy-start | bytes 55300
  82.0 9.2 %copy-start = (bf16[512,576]{0,1:T(8,128)(2,1)S(1)}, bf16[512,576]{0,1:T(8,128)(2,1)}, u32[]{:S(2)}) copy-start(bf16[512,576]{0,1:T(8,128)(2,1)} %param.13) | copy-start | bytes 1769476
  82.0 9.2 %copy-start.1 = (bf16[2048,576]{0,1:T(8,128)(2,1)S(1)}, bf16[2048,576]{0,1:T(8,128)(2,1)}, u32[]{:S(2)}) copy-start(bf16[2048,576]{0,1:T(8,128)(2,1)} %param.19) | copy-start | bytes 7077892

commit v4 on v3

--- a/solution.py
+++ b/solution.py
@@ -28,9 +28,9 @@
     ("sy", 3), ("sr", 1), ("g1", 2), ("sc", 3), ("M", 0), ("er", 2), ("se", 0), ("sz", 0), ("sr", 2),
     ("g1", 3), ("rot", 0), ("er", 3), ("se", 1), ("sz", 1), ("sr", 3), ("M", 1), ("M", 2), ("g3", 0),
     ("g3", 1), ("sp", 0), ("se", 2), ("sz", 2), ("M", 3), ("fin", 0), ("kv", 0), ("q", 0), ("se", 3),
-    ("sz", 3), ("sp", 1), ("sf", 0), ("g2", 2), ("M", 4), ("g2", 3), ("sp", 2), ("sf", 1), ("kt", 0),
-    ("M", 5), ("M", 6), ("sp", 3), ("sf", 2), ("k1", 0), ("sf", 3), ("g3", 2), ("k2", 0), ("g3", 3),
-    ("M", 7), ("fin", 1), ("kv", 1), ("q", 1), ("kt", 1), ("k1", 1), ("k2", 1),
+    ("sz", 3), ("sp", 1), ("sf", 0), ("g2", 2), ("M", 4), ("g2", 3), ("sp", 2), ("sf", 1), ("M", 5),
+    ("M", 6), ("sp", 3), ("kt", 0), ("g3", 2), ("g3", 3), ("M", 7), ("fin", 1), ("kv", 1), ("k1", 0),
+    ("sf", 2), ("sf", 3), ("q", 1), ("kt", 1), ("k2", 0), ("k1", 1), ("k2", 1),
 )
 F32 = jnp.float32
 BF16 = jnp.bfloat16

time: 117 us -> 112 us (0.957)
  Pallas kernels: 116 us -> 111 us
    pallas_call x1, Pallas kernels: 81.9 us -> 77.2 us  [on_device(): pl.pallas_call(kernel_in, out_shape=(jax.ShapeDtypeStruct((256, TOK), BF1...]
where the time goes in v4:
time: 112 us
  Pallas kernels  111 us (99%)
    pallas_call x1, Pallas kernels, on_device(): pl.pallas_call(kernel_in, out_shape=(jax.ShapeDtypeStruct((256, TOK), BF1...  77.2 us
    pallas_call x1, Pallas kernels, on_device(): pl.pallas_call(kernel_out, out_shape=jax.ShapeDtypeStruct((SHARD, TOK), B...  25.9 us
    pallas_call x1, Pallas kernels, on_device(): pl.pallas_call(kernel_attend, out_shape=jax.ShapeDtypeStruct((256, TOK),...  8.17 us

profile of v4, /device:TPU:2, one launch (start us, length us, event | category | flops | bytes accessed | tf_op | source)
XLA Modules:
  0.0 112.3 jit_solution(17509530009942163446)
XLA Ops:
  0.0 0.0 copy-start.2
  0.0 0.0 copy-start.3
  0.0 0.0 copy-start.4
  0.0 0.0 copy-start.5
  0.0 77.2 %shard_map.127 = (bf16[256,512]{1,0:T(8,128)(2,1)S(1)}, bf16[24,256,128]{2,1,0:T(8,128)(2,1)S(1)}, bf16[4,64,64,128]{3,2,1,0:T(8,128)(2,1)S(1)}) custom-call(s32[4]{0:T(128)} %owner_s.1, s32[1,48]{1,0:T(1,128)} %bitcast.14, s32[1,48]{1,0:T(1,128)} %bitcast.16, s32[1,48]{1,0:T(1,128)} %bitcast.18, f32[36,128]{1,0:T(8,128)} %bitcast.21, ...), custom_call_target="tpu_custom_call" | custom-call | tf_op jit(solution)/shard_map/pallas_call | solution.py:737
  77.2 0.0 copy-done.2
  77.2 0.0 copy-done.3
  77.2 0.0 copy-done.4
  77.2 0.0 copy-done.5
  77.3 0.0 copy-start.6
  77.3 0.0 copy-start
  77.3 0.0 copy-start.1
  77.3 8.2 %shard_map.128.att_ref = bf16[256,512]{1,0:T(8,128)(2,1)S(1)} custom-call(s32[4]{0:T(128)S(1)} %copy-done.5, s32[48]{0:T(128)S(1)} %copy-done.2, s32[48]{0:T(128)S(1)} %copy-done.3, s32[48]{0:T(128)S(1)} %copy-done.4, s32[1,48]{1,0:T(1,128)S(1)} %bitcast.15, s32[1,48]{1,0:T(1,128)S(1)} %bitcast.17, s32[1,48]{1,0:T(1,128)S(1)} %bitcast.19, ...), custom_call_target="tpu_custom_call" | custom-call | tf_op jit(solution)/shard_map/pallas_call | solution.py:771
  85.5 0.0 copy-done.6
  85.5 0.1 reshape.26
  85.6 0.0 copy-done
  85.6 0.0 copy-done.1
  85.6 25.9 %shard_map.129 = bf16[576,512]{1,0:T(8,128)(2,1)S(1)} custom-call(bf16[256,512]{1,0:T(8,128)(2,1)S(1)} %shard_map.128.att_ref, bf16[576,2048]{1,0:T(8,128)(2,1)S(1)} %bitcast.12, bf16[576,512]{1,0:T(8,128)(2,1)S(1)} %bitcast.11, f32[8,5,128]{2,1,0:T(8,128)S(1)} %copy.14.gain_ref), custom_call_target="tpu_custom_call" | custom-call | tf_op jit(solution)/shard_map/pallas_call | solution.py:785
  111.5 0.8 copy.16
  (2 shorter events, 0.0 us)
Async XLA Ops:
  0.0 77.2 %copy-start.2 = (s32[48]{0:T(128)S(1)}, s32[48]{0:T(128)}, u32[]{:S(2)}) copy-start(s32[48]{0:T(128)} %len_s.1) | copy-start | bytes 580
  0.0 77.2 %copy-start.3 = (s32[48]{0:T(128)S(1)}, s32[48]{0:T(128)}, u32[]{:S(2)}) copy-start(s32[48]{0:T(128)} %order_s.1) | copy-start | bytes 580
  0.0 77.2 %copy-start.4 = (s32[48]{0:T(128)S(1)}, s32[48]{0:T(128)}, u32[]{:S(2)}) copy-start(s32[48]{0:T(128)} %pref_s.1) | copy-start | bytes 580
  0.0 77.2 %copy-start.5 = (s32[4]{0:T(128)S(1)}, s32[4]{0:T(128)}, u32[]{:S(2)}) copy-start(s32[4]{0:T(128)} %owner_s.1) | copy-start | bytes 52
  77.3 8.2 %copy-start.6 = (f32[4608]{0:T(1024)S(1)}, f32[4608]{0:T(1024)}, u32[]{:S(2)}) copy-start(f32[4608]{0:T(1024)} %param.15) | copy-start | bytes 55300
  77.3 8.3 %copy-start = (bf16[512,576]{0,1:T(8,128)(2,1)S(1)}, bf16[512,576]{0,1:T(8,128)(2,1)}, u32[]{:S(2)}) copy-start(bf16[512,576]{0,1:T(8,128)(2,1)} %param.13) | copy-start | bytes 1769476
  77.3 8.3 %copy-start.1 = (bf16[2048,576]{0,1:T(8,128)(2,1)S(1)}, bf16[2048,576]{0,1:T(8,128)(2,1)}, u32[]{:S(2)}) copy-start(bf16[2048,576]{0,1:T(8,128)(2,1)} %param.19) | copy-start | bytes 7077892

commit v5 on v4

--- a/solution.py
+++ b/solution.py
@@ -16,8 +16,8 @@
 TOK = 512
 REQS = 48
 SHARD = 576
-IN_PIECES = (("P", "R"), ("P", "L"), ("P", "R"), ("P", "L"))
-OUT_PIECES = (("P", "R"), ("P", "L"), ("Q", "R"), ("Q", "L"))
+IN_PIECES = (("P", "R"), ("P", "L")) * 4
+OUT_PIECES = (("P", "R"), ("P", "L"), ("Q", "R"), ("Q", "L")) * 2
 SOFTCAP = 50.0
 EPS = 1e-6
 KEYS = 512
@@ -50,7 +50,8 @@
         self.count = 0
         self.started = []
         self.n = len(pieces)
-        self.prow = rows // 2 if halves else rows // self.n
+        self.per = self.n // 2
+        self.prow = rows // self.per if halves else rows // self.n
         self.halves = halves
 
     def target(self, way):
@@ -68,8 +69,8 @@
     def part(self, ref, base, k):
         if not self.halves:
             return ref.at[pl.ds(pl.multiple_of(base + k * self.prow, 16), self.prow)]
-        rows = pl.ds(pl.multiple_of(base + (k % 2) * self.prow, 16), self.prow)
-        return ref.at[rows, pl.ds((k // 2) * (TOK // 2), TOK // 2)]
+        rows = pl.ds(pl.multiple_of(base + (k % self.per) * self.prow, 16), self.prow)
+        return ref.at[rows, pl.ds((k // self.per) * (TOK // 2), TOK // 2)]
 
     def send(self, dx, dl, k, way):
         src = self.place(dx, dl, k)
@@ -196,7 +197,7 @@
     ]
     pl.semaphore_wait(barrier, len(peers))
     if "gather" in ON:
-        gather.start(0, 2)
+        gather.start(0, 4)
 
     to = lax.broadcasted_iota(jnp.int32, (256, 256), 0)
     of = lax.broadcasted_iota(jnp.int32, (256, 256), 1)
@@ -501,11 +502,18 @@
             kv_way(5, g, own, kv(3, g), sibling).wait_send()
             kv_way(6, g, own, kv(3, g), sibling).wait_send()
 
+    def both(step):
+        def run(k):
+            step(2 * k)
+            step(2 * k + 1)
+
+        return run
+
     steps = {
-        "W": turn_weights, "g1": gather.first, "g2": gather.second, "g3": gather.third, "sy": stage_y, "sc": stage_core,
+        "W": turn_weights, "g1": both(gather.first), "g2": both(gather.second), "g3": both(gather.third), "sy": stage_y, "sc": stage_core,
         "sr": stage_reduce, "er": stage_relay, "se": stage_end,
         "sz": stage_z, "sp": stage_spread, "sf": stage_far, "kt": kv_transit, "k1": kv_first, "k2": kv_second,
-        "rot": lambda _: rotary_tables(), "kv": kv_start, "fin": finish, "q": queries, "gs": lambda _: gather.start(2, 4),
+        "rot": lambda _: rotary_tables(), "kv": kv_start, "fin": finish, "q": queries, "gs": lambda _: gather.start(4, 8),
         "M": lambda i: multiply(
             (l * 2 + x // 2, l * 2 + 1 - x // 2, (1 - l) * 2 + x // 2, (1 - l) * 2 + 1 - x // 2)[i % 4], i // 4, i % 4 == 0
         ),
@@ -653,7 +661,7 @@
     wo_copy.start()
     own_copy.start()
     pl.semaphore_wait(barrier, 7)
-    gather.start(0, 4)
+    gather.start(0, gather.n)
 
     g5 = gain_ref[t]
     for b in range(5):
@@ -672,17 +680,17 @@
             acc[mm, :] = part if begin else acc[mm, :] + part
 
     multiply(0, 0, True)
-    for k in range(4):
+    for k in range(gather.n):
         gather.first(k)
     multiply(1, 0, False)
     multiply(3, 0, False)
     multiply(0, 1, False)
-    for k in range(4):
+    for k in range(gather.n):
         gather.second(k)
     multiply(2, 0, False)
     multiply(1, 1, False)
     multiply(3, 1, False)
-    for k in range(4):
+    for k in range(gather.n):
         gather.third(k)
     multiply(2, 1, False)
 

time: 112 us -> 113 us (level)
  no operation moved by 1% of the time
where the time goes in v5:
time: 113 us
  Pallas kernels  112 us (99%)
    pallas_call x1, Pallas kernels, on_device(): pl.pallas_call(kernel_in, out_shape=(jax.ShapeDtypeStruct((256, TOK), BF1...  76.8 us
    pallas_call x1, Pallas kernels, on_device(): pl.pallas_call(kernel_out, out_shape=jax.ShapeDtypeStruct((SHARD, TOK), B...  26 us
    pallas_call x1, Pallas kernels, on_device(): pl.pallas_call(kernel_attend, out_shape=jax.ShapeDtypeStruct((256, TOK),...  9.04 us

profile of v5, /device:TPU:2, one launch (start us, length us, event | category | flops | bytes accessed | tf_op | source)
XLA Modules:
  0.0 112.9 jit_solution(12371710062311905024)
XLA Ops:
  0.0 0.0 copy-start.2
  0.0 0.0 copy-start.3
  0.0 0.0 copy-start.4
  0.0 0.0 copy-start.5
  0.0 76.8 %shard_map.127 = (bf16[256,512]{1,0:T(8,128)(2,1)S(1)}, bf16[24,256,128]{2,1,0:T(8,128)(2,1)S(1)}, bf16[4,64,64,128]{3,2,1,0:T(8,128)(2,1)S(1)}) custom-call(s32[4]{0:T(128)} %owner_s.1, s32[1,48]{1,0:T(1,128)} %bitcast.14, s32[1,48]{1,0:T(1,128)} %bitcast.16, s32[1,48]{1,0:T(1,128)} %bitcast.18, f32[36,128]{1,0:T(8,128)} %bitcast.21, ...), custom_call_target="tpu_custom_call" | custom-call | tf_op jit(solution)/shard_map/pallas_call | solution.py:745
  76.8 0.0 copy-done.2
  76.8 0.0 copy-done.3
  76.8 0.0 copy-done.4
  76.9 0.0 copy-done.5
  76.9 0.0 copy-start.6
  76.9 0.0 copy-start
  76.9 0.0 copy-start.1
  76.9 9.0 %shard_map.128.att_ref = bf16[256,512]{1,0:T(8,128)(2,1)S(1)} custom-call(s32[4]{0:T(128)S(1)} %copy-done.5, s32[48]{0:T(128)S(1)} %copy-done.2, s32[48]{0:T(128)S(1)} %copy-done.3, s32[48]{0:T(128)S(1)} %copy-done.4, s32[1,48]{1,0:T(1,128)S(1)} %bitcast.15, s32[1,48]{1,0:T(1,128)S(1)} %bitcast.17, s32[1,48]{1,0:T(1,128)S(1)} %bitcast.19, ...), custom_call_target="tpu_custom_call" | custom-call | tf_op jit(solution)/shard_map/pallas_call | solution.py:779
  86.0 0.0 copy-done.6
  86.0 0.1 reshape.26
  86.1 0.0 copy-done
  86.1 0.0 copy-done.1
  86.1 26.0 %shard_map.129 = bf16[576,512]{1,0:T(8,128)(2,1)S(1)} custom-call(bf16[256,512]{1,0:T(8,128)(2,1)S(1)} %shard_map.128.att_ref, bf16[576,2048]{1,0:T(8,128)(2,1)S(1)} %bitcast.12, bf16[576,512]{1,0:T(8,128)(2,1)S(1)} %bitcast.11, f32[8,5,128]{2,1,0:T(8,128)S(1)} %copy.14.gain_ref), custom_call_target="tpu_custom_call" | custom-call | tf_op jit(solution)/shard_map/pallas_call | solution.py:793
  112.1 0.8 copy.16
  (2 shorter events, 0.0 us)
Async XLA Ops:
  0.0 76.8 %copy-start.2 = (s32[48]{0:T(128)S(1)}, s32[48]{0:T(128)}, u32[]{:S(2)}) copy-start(s32[48]{0:T(128)} %len_s.1) | copy-start | bytes 580
  0.0 76.8 %copy-start.3 = (s32[48]{0:T(128)S(1)}, s32[48]{0:T(128)}, u32[]{:S(2)}) copy-start(s32[48]{0:T(128)} %order_s.1) | copy-start | bytes 580
  0.0 76.8 %copy-start.4 = (s32[48]{0:T(128)S(1)}, s32[48]{0:T(128)}, u32[]{:S(2)}) copy-start(s32[48]{0:T(128)} %pref_s.1) | copy-start | bytes 580
  0.0 76.9 %copy-start.5 = (s32[4]{0:T(128)S(1)}, s32[4]{0:T(128)}, u32[]{:S(2)}) copy-start(s32[4]{0:T(128)} %owner_s.1) | copy-start | bytes 52
  76.9 9.1 %copy-start.6 = (f32[4608]{0:T(1024)S(1)}, f32[4608]{0:T(1024)}, u32[]{:S(2)}) copy-start(f32[4608]{0:T(1024)} %param.15) | copy-start | bytes 55300
  76.9 9.2 %copy-start = (bf16[512,576]{0,1:T(8,128)(2,1)S(1)}, bf16[512,576]{0,1:T(8,128)(2,1)}, u32[]{:S(2)}) copy-start(bf16[512,576]{0,1:T(8,128)(2,1)} %param.13) | copy-start | bytes 1769476
  76.9 9.2 %copy-start.1 = (bf16[2048,576]{0,1:T(8,128)(2,1)S(1)}, bf16[2048,576]{0,1:T(8,128)(2,1)}, u32[]{:S(2)}) copy-start(bf16[2048,576]{0,1:T(8,128)(2,1)} %param.19) | copy-start | bytes 7077892
